TPU v7x, 128 devices: a whole 4x4x4 slice. The times are simulated.
128 devices in a mesh: row: 8 (over y, core), col: 16 (over x, z).
Axes of the slice: x: 4, y: 4, z: 4, core: 2. Of those that a mesh axis runs over, the one named last changes fastest.
Arguments:
- jacobian: bfloat16 [256, 65536], P(('row', 'col')), may hold values from -0.25 to 0.25
- curvature: float32 [256], P(('row', 'col')), may hold values from 0.1 to 10
- sub_index: int32 [65536], P(('row', 'col')), may hold values from 0 to 4194303, as said below
- prior_precision: float32 [32], replicated, may hold values from 0.5 to 4
Outputs:
- factored: float32 [128, 8, 512, 512], P(('row', 'col'))
Inputs may be any that keep to these rules, and one draw needn't show every extreme that they name: `sub_index`: strictly increasing along the weights, so each tile holds nearby weights; the first is 0 and the last is 4194303.
All inputs are finite; a program needn't handle non-finite values.
Results may differ from a plain program's by a relative error of at most 0.0025.
Values may be sent and summed in bfloat16 or wider, within the bound.
No kernel may reach another device: no remote copies, remote signals or barrier semaphores. Data moves between devices by JAX's collectives and lax.ppermute only.
A program may use at most 128 MiB of HBM per device.

v0:
```python
import jax
import jax.numpy as jnp
from jax import lax
from jax.sharding import PartitionSpec as P

TILE = 512
TILES_DEV = 1
BAND = 8
LAYERS = 32
SPAN = 131072


def shifted(shard, axis, by):
    length = lax.axis_size(axis)
    pairs = [(i, i + by) for i in range(length) if 0 <= i + by < length]
    return lax.ppermute(shard, axis, pairs)


def earlier_tiles(own_tiles):
    reach_count = BAND // TILES_DEV - 1
    pieces = []
    for distance in range(1, reach_count + 1):
        pieces.append(shifted(own_tiles, ("row", "col"), distance))
    return jnp.concatenate(pieces[::-1] + [own_tiles], axis=1)


def earlier_slices(own_slices):
    reach_count = BAND // TILES_DEV - 1
    pieces = []
    for distance in range(1, reach_count + 1):
        pieces.append(shifted(own_slices, ("row", "col"), distance))
    return jnp.concatenate(pieces[::-1] + [own_slices], axis=0)


def band_of_rows(blocks, local_row):
    return blocks[local_row, :, local_row : local_row + BAND, :][:, ::-1, :].transpose(1, 0, 2)


def body(jacobian, curvature, sub_index, prior_precision):
    scaled = (jnp.sqrt(curvature)[:, None] * jacobian.astype(jnp.float32)).astype(jnp.bfloat16)
    columns = lax.all_to_all(scaled, ("row", "col"), split_axis=1, concat_axis=0, tiled=True)
    position = lax.axis_index(("row", "col"))
    first_row = position * TILES_DEV
    row_ids = first_row + jnp.arange(TILES_DEV, dtype=jnp.int32)
    band_index = jnp.arange(BAND, dtype=jnp.int32)
    gram_window = earlier_tiles(columns)
    product = lax.dot_general(
        columns, gram_window, (((0,), (0,)), ((), ())), preferred_element_type=jnp.float32
    )
    blocks = product.reshape(TILES_DEV, TILE, BAND, TILE)
    band_tiles = jnp.stack([band_of_rows(blocks, 0)])
    in_group = band_index[None, :] <= (row_ids % BAND)[:, None]
    band_tiles = jnp.where(in_group[:, :, None, None], band_tiles, jnp.float32(0.0))
    layer_ids = sub_index // SPAN
    anchor = jnp.sum(
        jnp.where(
            layer_ids[:, None] == jnp.arange(LAYERS, dtype=jnp.int32)[None, :],
            prior_precision[None, :],
            jnp.float32(0.0),
        ),
        axis=1,
    )
    anchor = anchor.reshape(TILES_DEV, TILE)
    identity = jnp.eye(TILE, dtype=jnp.float32)
    band_tiles = band_tiles.at[:, 0].add(identity[None] * anchor[:, :, None])
    group_start = first_row // BAND * BAND
    window_ids = first_row - (BAND - TILES_DEV) + band_index
    pivot_row = group_start + 0
    offsets = row_ids - pivot_row
    in_band = offsets >= 0
    clipped = jnp.clip(offsets, 0, BAND - 1)
    own_slices = jnp.stack([lax.dynamic_index_in_dim(band_tiles[0], clipped[0], 0, keepdims=False)])
    own_slices = jnp.where(in_band[:, None, None], own_slices, jnp.float32(0.0))
    window_slices = earlier_slices(own_slices)
    window_slices = jnp.where(
        (window_ids >= pivot_row)[:, None, None], window_slices, jnp.float32(0.0)
    )
    diag_pos = pivot_row - first_row + BAND - TILES_DEV
    diag_ok = (diag_pos >= 0) & (diag_pos < BAND)
    pivot_tile = lax.dynamic_index_in_dim(
        window_slices, jnp.clip(diag_pos, 0, BAND - 1), 0, keepdims=False
    )
    pivot_tile = jnp.where(diag_ok, pivot_tile, identity)
    factor_tile = jnp.linalg.cholesky(pivot_tile)
    solved = lax.linalg.triangular_solve(
        factor_tile,
        window_slices.reshape(BAND * TILE, TILE),
        left_side=False,
        lower=True,
        transpose_a=True,
    )
    own_solved = solved[(BAND - TILES_DEV) * TILE :]
    update = jnp.dot(
        own_solved, solved.T, precision=lax.Precision.HIGHEST, preferred_element_type=jnp.float32
    )
    update = update.reshape(TILES_DEV, TILE, BAND, TILE)
    row_now = row_ids[0]
    below_mask = row_now - band_index > pivot_row
    picked = band_of_rows(update, 0)
    row_tiles = band_tiles[0] - jnp.where(below_mask[:, None, None], picked, jnp.float32(0.0))
    written = jnp.where(row_now == pivot_row, factor_tile, own_solved)
    target_mask = band_index == row_now - pivot_row
    row_tiles = jnp.where(target_mask[:, None, None], written[None], row_tiles)
    new_rows = [row_tiles]
    band_tiles = jnp.stack(new_rows)
    return band_tiles


def solution(mesh):
    placed = (P(("row", "col"), None), P(("row", "col")), P(("row", "col")), P())
    return jax.shard_map(
        body,
        mesh=mesh,
        in_specs=placed,
        out_specs=P(("row", "col"), None, None, None),
        check_vma=False,
    )
```

profile of v0, /device:TPU:2, one launch (start us, length us, event | category | flops | bytes accessed | tf_op | source)
XLA Modules:
  0.0 467.6 jit_solution(8679863758297217116)
XLA Ops:
  1.9 20.8 %all_to_all.19 = bf16[2,128,512]{2,0,1:T(2,128)(2,1)S(1)} all-to-all(bf16[2,128,512]{2,0,1:T(2,128)(2,1)S(1)} %bitcast.81), channel_id=1, replica_groups=mesh['row'=8,'col'=16] {'row','col'}, dimensions={1} | all-to-all | bytes 524288 | tf_op jit(solution)/shard_map/all_to_all | solution.py:41
  22.8 2.3 collective-permute-start
  25.8 5.2 %collective-permute-start.1 = (bf16[256,512]{1,0:T(8,128)(2,1)S(1)}, bf16[256,512]{1,0:T(8,128)(2,1)S(1)}, u32[]{:S(2)}, u32[]{:S(2)}) collective-permute-start(bf16[256,512]{1,0:T(8,128)(2,1)S(1)} %all_to_all.17), channel_id=1, source_target_pairs={{0,6},{1,7},{2,8},{3,9},{4,10},{5,11},{6,12},{7,13},{8,14},{9,15},... | collective-permute-start | bytes 786440 | tf_op jit(solution)/shard_map/ppermute | solution.py:16
  31.8 2.5 collective-permute-start.2
  34.3 2.9 collective-permute-start.3
  37.2 4.9 %collective-permute-start.4 = (bf16[256,512]{1,0:T(8,128)(2,1)S(1)}, bf16[256,512]{1,0:T(8,128)(2,1)S(1)}, u32[]{:S(2)}, u32[]{:S(2)}) collective-permute-start(bf16[256,512]{1,0:T(8,128)(2,1)S(1)} %all_to_all.17), channel_id=1, source_target_pairs={{0,3},{1,4},{2,5},{3,6},{4,7},{5,8},{6,9},{7,10},{8,11},{9,12},{10... | collective-permute-start | bytes 786440 | tf_op jit(solution)/shard_map/ppermute | solution.py:16
  42.1 3.3 collective-permute-start.5
  45.4 4.8 %collective-permute-start.6 = (bf16[256,512]{1,0:T(8,128)(2,1)S(1)}, bf16[256,512]{1,0:T(8,128)(2,1)S(1)}, u32[]{:S(2)}, u32[]{:S(2)}) collective-permute-start(bf16[256,512]{1,0:T(8,128)(2,1)S(1)} %all_to_all.17), channel_id=1, source_target_pairs={{0,1},{1,2},{2,3},{3,4},{4,5},{5,6},{6,7},{7,8},{8,9},{9,10},{10,1... | collective-permute-start | bytes 786440 | tf_op jit(solution)/shard_map/ppermute | solution.py:16
  50.3 6.4 %collective-permute-done.4 = bf16[256,512]{1,0:T(8,128)(2,1)S(1)} collective-permute-done((bf16[256,512]{1,0:T(8,128)(2,1)S(1)}, bf16[256,512]{1,0:T(8,128)(2,1)S(1)}, u32[]{:S(2)}, u32[]{:S(2)}) %collective-permute-start.4) | collective-permute-done | bytes 262176 | tf_op jit(solution)/shard_map/ppermute | solution.py:16
  56.8 6.4 %collective-permute-done.5 = bf16[256,512]{1,0:T(8,128)(2,1)S(1)} collective-permute-done((bf16[256,512]{1,0:T(8,128)(2,1)S(1)}, bf16[256,512]{1,0:T(8,128)(2,1)S(1)}, u32[]{:S(2)}, u32[]{:S(2)}) %collective-permute-start.5) | collective-permute-done | bytes 262176 | tf_op jit(solution)/shard_map/ppermute | solution.py:16
  63.2 6.4 %collective-permute-done.6 = bf16[256,512]{1,0:T(8,128)(2,1)S(1)} collective-permute-done((bf16[256,512]{1,0:T(8,128)(2,1)S(1)}, bf16[256,512]{1,0:T(8,128)(2,1)S(1)}, u32[]{:S(2)}, u32[]{:S(2)}) %collective-permute-start.6) | collective-permute-done | bytes 262176 | tf_op jit(solution)/shard_map/ppermute | solution.py:16
  71.0 3.3 copy.24
  77.4 3.4 copy-done
  83.4 2.3 collective-permute-start.8
  85.7 5.9 %collective-permute-start.9 = (f32[1,512,512]{2,1,0:T(8,128)}, f32[1,512,512]{2,1,0:T(8,128)}, u32[]{:S(2)}, u32[]{:S(2)}) collective-permute-start(f32[1,512,512]{2,1,0:T(8,128)} %dynamic-slice_select_fusion.1), channel_id=1, source_target_pairs={{0,5},{1,6},{2,7},{3,8},{4,9},{5,10},{6,11},{7,12},{8,13},{9,14},{... | collective-permute-start | bytes 3145736 | tf_op jit(solution)/shard_map/ppermute | solution.py:16
  91.6 2.7 collective-permute-start.10
  94.3 5.3 %collective-permute-start.11 = (f32[1,512,512]{2,1,0:T(8,128)}, f32[1,512,512]{2,1,0:T(8,128)S(1)}, u32[]{:S(2)}, u32[]{:S(2)}) collective-permute-start(f32[1,512,512]{2,1,0:T(8,128)} %dynamic-slice_select_fusion.1), channel_id=1, source_target_pairs={{0,3},{1,4},{2,5},{3,6},{4,7},{5,8},{6,9},{7,10},{8,11},{9,12},{10... | collective-permute-start | bytes 3145736 | tf_op jit(solution)/shard_map/ppermute | solution.py:16
  100.2 7.1 %collective-permute-done.7 = f32[1,512,512]{2,1,0:T(8,128)S(1)} collective-permute-done((f32[1,512,512]{2,1,0:T(8,128)}, f32[1,512,512]{2,1,0:T(8,128)S(1)}, u32[]{:S(2)}, u32[]{:S(2)}) %collective-permute-start.7) | collective-permute-done | bytes 1048608 | tf_op jit(solution)/shard_map/ppermute | solution.py:16
  109.3 20.5 %collective-permute-done.8 = f32[1,512,512]{2,1,0:T(8,128)} collective-permute-done((f32[1,512,512]{2,1,0:T(8,128)}, f32[1,512,512]{2,1,0:T(8,128)}, u32[]{:S(2)}, u32[]{:S(2)}) %collective-permute-start.8) | collective-permute-done | bytes 1048608 | tf_op jit(solution)/shard_map/ppermute | solution.py:16
  129.8 6.4 %collective-permute-start.13 = (f32[1,512,512]{2,1,0:T(8,128)}, f32[1,512,512]{2,1,0:T(8,128)S(1)}, u32[]{:S(2)}, u32[]{:S(2)}) collective-permute-start(f32[1,512,512]{2,1,0:T(8,128)} %dynamic-slice_select_fusion.1), channel_id=1, source_target_pairs={{0,1},{1,2},{2,3},{3,4},{4,5},{5,6},{6,7},{7,8},{8,9},{9,10},{10,1... | collective-permute-start | bytes 3145736 | tf_op jit(solution)/shard_map/ppermute | solution.py:16
  137.6 14.6 %collective-permute-done.9 = f32[1,512,512]{2,1,0:T(8,128)} collective-permute-done((f32[1,512,512]{2,1,0:T(8,128)}, f32[1,512,512]{2,1,0:T(8,128)}, u32[]{:S(2)}, u32[]{:S(2)}) %collective-permute-start.9) | collective-permute-done | bytes 1048608 | tf_op jit(solution)/shard_map/ppermute | solution.py:16
  153.6 22.3 %collective-permute-done.10 = f32[1,512,512]{2,1,0:T(8,128)S(1)} collective-permute-done((f32[1,512,512]{2,1,0:T(8,128)}, f32[1,512,512]{2,1,0:T(8,128)S(1)}, u32[]{:S(2)}, u32[]{:S(2)}) %collective-permute-start.10) | collective-permute-done | bytes 1048608 | tf_op jit(solution)/shard_map/ppermute | solution.py:16
  175.9 26.7 %collective-permute-done.11 = f32[1,512,512]{2,1,0:T(8,128)S(1)} collective-permute-done((f32[1,512,512]{2,1,0:T(8,128)}, f32[1,512,512]{2,1,0:T(8,128)S(1)}, u32[]{:S(2)}, u32[]{:S(2)}) %collective-permute-start.11) | collective-permute-done | bytes 1048608 | tf_op jit(solution)/shard_map/ppermute | solution.py:16
  202.7 16.8 %collective-permute-done.12 = f32[1,512,512]{2,1,0:T(8,128)} collective-permute-done((f32[1,512,512]{2,1,0:T(8,128)}, f32[1,512,512]{2,1,0:T(8,128)}, u32[]{:S(2)}, u32[]{:S(2)}) %collective-permute-start.12) | collective-permute-done | bytes 1048608 | tf_op jit(solution)/shard_map/ppermute | solution.py:16
  220.8 21.0 %collective-permute-done.13 = f32[1,512,512]{2,1,0:T(8,128)S(1)} collective-permute-done((f32[1,512,512]{2,1,0:T(8,128)}, f32[1,512,512]{2,1,0:T(8,128)S(1)}, u32[]{:S(2)}, u32[]{:S(2)}) %collective-permute-start.13) | collective-permute-done | bytes 1048608 | tf_op jit(solution)/shard_map/ppermute | solution.py:16
  243.2 3.2 copy-done.7
  248.1 11.7 %cholesky.104 = f32[128,128]{1,0:T(8,128)S(1)} custom-call(f32[128,128]{1,0:T(8,128)S(1)} %cholesky.266), custom_call_target="Cholesky" | custom-call | tf_op jit(solution)/shard_map/jit(cholesky)/cholesky | solution.py:84
  260.0 9.8 %custom-call.30 = f32[1,128,128]{1,2,0:T(8,128)S(1)} custom-call(f32[1,128,128]{2,1,0:T(8,128)S(1)} %get-tuple-element.44), custom_call_target="InvertDiagBlocksLowerTriangular" | custom-call | tf_op jit(solution)/shard_map/jit(cholesky)/cholesky | solution.py:84
  270.5 11.9 %cholesky.217 = f32[128,128]{1,0:T(8,128)S(1)} custom-call(f32[128,128]{1,0:T(8,128)S(1)} %cholesky.270), custom_call_target="Cholesky" | custom-call | tf_op jit(solution)/shard_map/jit(cholesky)/cholesky | solution.py:84
  283.7 9.8 %custom-call.31 = f32[1,128,128]{1,2,0:T(8,128)S(1)} custom-call(f32[1,128,128]{2,1,0:T(8,128)S(1)} %get-tuple-element.41), custom_call_target="InvertDiagBlocksLowerTriangular" | custom-call | tf_op jit(solution)/shard_map/jit(cholesky)/cholesky | solution.py:84
  294.2 11.7 %cholesky.238 = f32[128,128]{1,0:T(8,128)S(1)} custom-call(f32[128,128]{1,0:T(8,128)S(1)} %cholesky.275), custom_call_target="Cholesky" | custom-call | tf_op jit(solution)/shard_map/jit(cholesky)/cholesky | solution.py:84
  306.6 9.8 %custom-call.32 = f32[1,128,128]{1,2,0:T(8,128)S(1)} custom-call(f32[1,128,128]{2,1,0:T(8,128)S(1)} %get-tuple-element.38), custom_call_target="InvertDiagBlocksLowerTriangular" | custom-call | tf_op jit(solution)/shard_map/jit(cholesky)/cholesky | solution.py:84
  317.0 12.1 %cholesky.255 = f32[128,128]{1,0:T(8,128)S(1)} custom-call(f32[128,128]{1,0:T(8,128)S(1)} %convolution_subtract_fusion.2), custom_call_target="Cholesky" | custom-call | tf_op jit(solution)/shard_map/jit(cholesky)/cholesky | solution.py:84
  332.3 10.1 %while.2 = (s32[]{:T(128)}, f32[512,512]{1,0:T(8,128)S(1)}, s32[4,2]{0,1:T(2,128)S(1)}, f32[4,128,128]{2,1,0:T(8,128)}, s32[]{:T(128)}) while((s32[]{:T(128)}, f32[512,512]{1,0:T(8,128)S(1)}, s32[4,2]{0,1:T(2,128)S(1)}, f32[4,128,128]{2,1,0:T(8,128)}, s32[]{:T(128)}) %tuple.31), condition=%wide.while_cond.1, body=%wide.while_body.1.sunk | while | flops 2 | bytes 132705 | solution.py:85
  342.4 40.2 %custom-call.33 = f32[4,128,128]{1,2,0:T(8,128)S(1)} custom-call(f32[4,128,128]{2,1,0:T(8,128)} %get-tuple-element.24), custom_call_target="InvertDiagBlocksLowerTriangular" | custom-call | tf_op jit(solution)/shard_map/triangular_solve | solution.py:85
  382.6 3.9 bitcast_select_fusion
  386.5 2.0 fusion.23
  388.5 4.5 fusion.39
  393.0 2.1 fusion.22
  395.1 8.2 %fusion.16 = f32[4096,128]{1,0:T(8,128)S(1)} fusion(f32[4096,128]{0,1:T(8,128)S(1)} %fusion.22, f32[4096,128]{0,1:T(8,128)S(1)} %fusion.23, f32[512,512]{1,0:T(8,128)} %copy-done.8), kind=kOutput, calls=%fused_computation.21 | convolution fusion | flops 1611661312 | bytes 6422528 | tf_op jit(solution)/shard_map/triangular_solve | solution.py:85
  403.3 2.1 fusion.21
  406.8 12.5 %fusion.10 = f32[4096,128]{1,0:T(8,128)} fusion(f32[4096,128]{0,1:T(8,128)S(1)} %fusion.21, f32[4096,128]{0,1:T(8,128)S(1)} %fusion.22, f32[4096,128]{0,1:T(8,128)S(1)} %fusion.23, f32[512,512]{1,0:T(8,128)} %copy-done.8), kind=kOutput, calls=%fused_computation.15 | convolution fusion | flops 2419064832 | bytes 8585216 | tf_op jit(solution)/shard_map/triangular_solve | solution.py:85
  419.3 2.9 copy.30
  422.2 2.9 copy.29
  427.0 3.7 fusion.20
  431.1 15.5 %fusion = f32[512,4096]{0,1:T(8,128)} fusion(f32[4096,128]{1,0:T(8,128)S(1)} %fusion.20, f32[4096,128]{1,0:T(8,128)S(1)} %copy-done.3, f32[4096,128]{1,0:T(8,128)S(1)} %copy-done.4, f32[4096,128]{1,0:T(8,128)S(1)} %copy-done.5), kind=kOutput, calls=%fused_computation.2 | convolution fusion | flops 12891979776 | bytes 16777216 | tf_op jit(solution)/shard_map/dot_general | solution.py:93
  446.8 9.1 %copy.33 = f32[512,8,512]{2,0,1:T(8,128)} copy(f32[512,8,512]{0,2,1:T(8,128)} %bitcast.78) | data formatting | bytes 16777216 | tf_op jit(solution)/shard_map/squeeze;reshape | solution.py:36
  455.9 11.5 %fusion.9 = f32[1,8,512,512]{3,2,1,0:T(8,128)} fusion(f32[8,512,512]{2,1,0:T(8,128)} %copy-done, f32[512,8,512]{2,0,1:T(8,128)} %copy.33, f32[512,512]{1,0:T(8,128)S(1)} %fusion.25, pred[8]{0:T(512)(128)(4,1)S(1)} %get-tuple-element.47, pred[8]{0:T(512)(128)(4,1)S(1)} %iota_compare_fusion.7), kind=kLoop, calls=%fused_computation.12 | loop fusion | flops 6291456 | bytes 26214416 | tf_op jit(solution)/shard_map/stack | solution.py:105
  (96 shorter events, 39.1 us)
Async XLA Ops:
  22.8 19.3 %collective-permute-start = (bf16[256,512]{1,0:T(8,128)(2,1)S(1)}, bf16[256,512]{1,0:T(8,128)(2,1)S(1)}, u32[]{:S(2)}, u32[]{:S(2)}) collective-permute-start(bf16[256,512]{1,0:T(8,128)(2,1)S(1)} %all_to_all.17), channel_id=1, source_target_pairs={{0,7},{1,8},{2,9},{3,10},{4,11},{5,12},{6,13},{7,14},{8,15},{9,16}... | collective-permute-start | bytes 786440 | tf_op jit(solution)/shard_map/ppermute | solution.py:16
  25.8 19.6 %collective-permute-start.1 = (bf16[256,512]{1,0:T(8,128)(2,1)S(1)}, bf16[256,512]{1,0:T(8,128)(2,1)S(1)}, u32[]{:S(2)}, u32[]{:S(2)}) collective-permute-start(bf16[256,512]{1,0:T(8,128)(2,1)S(1)} %all_to_all.17), channel_id=1, source_target_pairs={{0,6},{1,7},{2,8},{3,9},{4,10},{5,11},{6,12},{7,13},{8,14},{9,15},... | collective-permute-start | bytes 786440 | tf_op jit(solution)/shard_map/ppermute | solution.py:16
  31.8 18.5 %collective-permute-start.2 = (bf16[256,512]{1,0:T(8,128)(2,1)S(1)}, bf16[256,512]{1,0:T(8,128)(2,1)S(1)}, u32[]{:S(2)}, u32[]{:S(2)}) collective-permute-start(bf16[256,512]{1,0:T(8,128)(2,1)S(1)} %all_to_all.17), channel_id=1, source_target_pairs={{0,5},{1,6},{2,7},{3,8},{4,9},{5,10},{6,11},{7,12},{8,13},{9,14},{... | collective-permute-start | bytes 786440 | tf_op jit(solution)/shard_map/ppermute | solution.py:16
  34.3 16.0 %collective-permute-start.3 = (bf16[256,512]{1,0:T(8,128)(2,1)S(1)}, bf16[256,512]{1,0:T(8,128)(2,1)S(1)}, u32[]{:S(2)}, u32[]{:S(2)}) collective-permute-start(bf16[256,512]{1,0:T(8,128)(2,1)S(1)} %all_to_all.17), channel_id=1, source_target_pairs={{0,4},{1,5},{2,6},{3,7},{4,8},{5,9},{6,10},{7,11},{8,12},{9,13},{1... | collective-permute-start | bytes 786440 | tf_op jit(solution)/shard_map/ppermute | solution.py:16
  37.2 19.5 %collective-permute-start.4 = (bf16[256,512]{1,0:T(8,128)(2,1)S(1)}, bf16[256,512]{1,0:T(8,128)(2,1)S(1)}, u32[]{:S(2)}, u32[]{:S(2)}) collective-permute-start(bf16[256,512]{1,0:T(8,128)(2,1)S(1)} %all_to_all.17), channel_id=1, source_target_pairs={{0,3},{1,4},{2,5},{3,6},{4,7},{5,8},{6,9},{7,10},{8,11},{9,12},{10... | collective-permute-start | bytes 786440 | tf_op jit(solution)/shard_map/ppermute | solution.py:16
  42.1 21.0 %collective-permute-start.5 = (bf16[256,512]{1,0:T(8,128)(2,1)S(1)}, bf16[256,512]{1,0:T(8,128)(2,1)S(1)}, u32[]{:S(2)}, u32[]{:S(2)}) collective-permute-start(bf16[256,512]{1,0:T(8,128)(2,1)S(1)} %all_to_all.17), channel_id=1, source_target_pairs={{0,2},{1,3},{2,4},{3,5},{4,6},{5,7},{6,8},{7,9},{8,10},{9,11},{10,... | collective-permute-start | bytes 786440 | tf_op jit(solution)/shard_map/ppermute | solution.py:16
  45.4 24.2 %collective-permute-start.6 = (bf16[256,512]{1,0:T(8,128)(2,1)S(1)}, bf16[256,512]{1,0:T(8,128)(2,1)S(1)}, u32[]{:S(2)}, u32[]{:S(2)}) collective-permute-start(bf16[256,512]{1,0:T(8,128)(2,1)S(1)} %all_to_all.17), channel_id=1, source_target_pairs={{0,1},{1,2},{2,3},{3,4},{4,5},{5,6},{6,7},{7,8},{8,9},{9,10},{10,1... | collective-permute-start | bytes 786440 | tf_op jit(solution)/shard_map/ppermute | solution.py:16
  69.6 1.3 copy-start.9
  77.4 3.4 copy-start
  81.9 25.4 %collective-permute-start.7 = (f32[1,512,512]{2,1,0:T(8,128)}, f32[1,512,512]{2,1,0:T(8,128)S(1)}, u32[]{:S(2)}, u32[]{:S(2)}) collective-permute-start(f32[1,512,512]{2,1,0:T(8,128)} %dynamic-slice_select_fusion.1), channel_id=1, source_target_pairs={{0,7},{1,8},{2,9},{3,10},{4,11},{5,12},{6,13},{7,14},{8,15},{9,16}... | collective-permute-start | bytes 3145736 | tf_op jit(solution)/shard_map/ppermute | solution.py:16
  83.4 46.4 %collective-permute-start.8 = (f32[1,512,512]{2,1,0:T(8,128)}, f32[1,512,512]{2,1,0:T(8,128)}, u32[]{:S(2)}, u32[]{:S(2)}) collective-permute-start(f32[1,512,512]{2,1,0:T(8,128)} %dynamic-slice_select_fusion.1), channel_id=1, source_target_pairs={{0,6},{1,7},{2,8},{3,9},{4,10},{5,11},{6,12},{7,13},{8,14},{9,15},... | collective-permute-start | bytes 3145736 | tf_op jit(solution)/shard_map/ppermute | solution.py:16
  85.7 66.6 %collective-permute-start.9 = (f32[1,512,512]{2,1,0:T(8,128)}, f32[1,512,512]{2,1,0:T(8,128)}, u32[]{:S(2)}, u32[]{:S(2)}) collective-permute-start(f32[1,512,512]{2,1,0:T(8,128)} %dynamic-slice_select_fusion.1), channel_id=1, source_target_pairs={{0,5},{1,6},{2,7},{3,8},{4,9},{5,10},{6,11},{7,12},{8,13},{9,14},{... | collective-permute-start | bytes 3145736 | tf_op jit(solution)/shard_map/ppermute | solution.py:16
  91.6 84.2 %collective-permute-start.10 = (f32[1,512,512]{2,1,0:T(8,128)}, f32[1,512,512]{2,1,0:T(8,128)S(1)}, u32[]{:S(2)}, u32[]{:S(2)}) collective-permute-start(f32[1,512,512]{2,1,0:T(8,128)} %dynamic-slice_select_fusion.1), channel_id=1, source_target_pairs={{0,4},{1,5},{2,6},{3,7},{4,8},{5,9},{6,10},{7,11},{8,12},{9,13},{1... | collective-permute-start | bytes 3145736 | tf_op jit(solution)/shard_map/ppermute | solution.py:16
  94.3 108.4 %collective-permute-start.11 = (f32[1,512,512]{2,1,0:T(8,128)}, f32[1,512,512]{2,1,0:T(8,128)S(1)}, u32[]{:S(2)}, u32[]{:S(2)}) collective-permute-start(f32[1,512,512]{2,1,0:T(8,128)} %dynamic-slice_select_fusion.1), channel_id=1, source_target_pairs={{0,3},{1,4},{2,5},{3,6},{4,7},{5,8},{6,9},{7,10},{8,11},{9,12},{10... | collective-permute-start | bytes 3145736 | tf_op jit(solution)/shard_map/ppermute | solution.py:16
  107.3 112.2 %collective-permute-start.12 = (f32[1,512,512]{2,1,0:T(8,128)}, f32[1,512,512]{2,1,0:T(8,128)}, u32[]{:S(2)}, u32[]{:S(2)}) collective-permute-start(f32[1,512,512]{2,1,0:T(8,128)} %dynamic-slice_select_fusion.1), channel_id=1, source_target_pairs={{0,2},{1,3},{2,4},{3,5},{4,6},{5,7},{6,8},{7,9},{8,10},{9,11},{10,... | collective-permute-start | bytes 3145736 | tf_op jit(solution)/shard_map/ppermute | solution.py:16
  129.8 112.0 %collective-permute-start.13 = (f32[1,512,512]{2,1,0:T(8,128)}, f32[1,512,512]{2,1,0:T(8,128)S(1)}, u32[]{:S(2)}, u32[]{:S(2)}) collective-permute-start(f32[1,512,512]{2,1,0:T(8,128)} %dynamic-slice_select_fusion.1), channel_id=1, source_target_pairs={{0,1},{1,2},{2,3},{3,4},{4,5},{5,6},{6,7},{7,8},{8,9},{9,10},{10,1... | collective-permute-start | bytes 3145736 | tf_op jit(solution)/shard_map/ppermute | solution.py:16
  243.2 3.2 copy-start.7
  342.4 40.2 %copy-start.8 = (f32[512,512]{1,0:T(8,128)}, f32[512,512]{1,0:T(8,128)S(1)}, u32[]{:S(2)}) copy-start(f32[512,512]{1,0:T(8,128)S(1)} %get-tuple-element.93) | copy-start | bytes 3145732
  386.5 16.8 %copy-start.1 = (f32[4096,512]{1,0:T(8,128)}, f32[4096,512]{1,0:T(8,128)S(1)}, u32[]{:S(2)}) copy-start(f32[4096,512]{1,0:T(8,128)S(1)} %bitcast_select_fusion) | copy-start | bytes 25165828
  395.1 10.3 %copy-start.2 = (f32[4096,128]{0,1:T(8,128)}, f32[4096,128]{0,1:T(8,128)S(1)}, u32[]{:S(2)}) copy-start(f32[4096,128]{0,1:T(8,128)S(1)} %fusion.22) | copy-start | bytes 6291460
  405.5 1.3 copy-start.6
  426.9 3.7 copy-start.3
  427.0 3.7 copy-start.4
  427.0 4.2 copy-start.5
where the time goes:
time: 476 us; the launch traced here: 468 us
  waiting for transfers between devices  148 us (31%)
  other arithmetic  143 us (30%)
  matrix products  53.8 us (11%)
  starting transfers between devices  51.7 us (11%)
  local copies, waits for them, and re-layouts  46.3 us (10%)
  blocking collectives  20.8 us (4%)
    ppermute x14, waiting for transfers between devices, shifted(): return lax.ppermute(shard, axis, pairs)  148 us
    another operation x15, other arithmetic, body(): factor_tile = jnp.linalg.cholesky(pivot_tile)  79.6 us
    ppermute x14, starting transfers between devices, shifted(): return lax.ppermute(shard, axis, pairs)  51.7 us
    another operation x3, other arithmetic, body(): lax.linalg.triangular_solve(factor_tile, window_slices.reshape(BAND * TIL...  40.3 us
    another operation x7, matrix products, body(): lax.linalg.triangular_solve(factor_tile, window_slices.reshape(BAND * TIL...  35.1 us
    all_to_all x1, blocking collectives, body(): lax.all_to_all(scaled, ('row', 'col'), split_axis=1, concat_axis=0, tiled...  20.8 us
    dot_general x1, matrix products, body(): jnp.dot(own_solved, solved.T, precision=lax.Precision.HIGHEST, preferred_...  15.5 us
    unnamed x36, local copies, waits for them, and re-layouts  14.1 us
  transfers between devices with their start and end apart: 14, of which 10 were waited for; matrix products, arithmetic and copies ran while one was open for 1% of the time, Pallas kernels for 0%

commit v1 on v0

v1 whole, which is shorter than its diff:
```python
import jax
import jax.numpy as jnp
from jax import lax
from jax.experimental import pallas as pl
from jax.experimental.pallas import tpu as pltpu
from jax.sharding import PartitionSpec as P

TILE = 512
BAND = 8
LAYERS = 32
SPAN = 131072
GROUPS = 16
DEVICES = 128
EXAMPLES = 256
WIDE = TILE + 128
REST = (BAND - 1) * TILE
PART = 128
F32 = jnp.float32
BF16 = jnp.bfloat16
AXES = ("row", "col")
VMEM_LIMIT = 56 * 1024 * 1024


def params():
    return pltpu.CompilerParams(vmem_limit_bytes=VMEM_LIMIT)


def halves(x):
    high = x.astype(BF16)
    return high, (x - high.astype(F32)).astype(BF16)


def thirds(x):
    high = x.astype(BF16)
    rest = x - high.astype(F32)
    mid = rest.astype(BF16)
    return high, mid, (rest - mid.astype(F32)).astype(BF16)


def dot(a, b, contract):
    return lax.dot_general(a, b, ((contract[0], contract[1]), ((), ())), preferred_element_type=F32)


def dot_full(a, b, contract):
    return lax.dot_general(
        a, b, ((contract[0], contract[1]), ((), ())),
        precision=lax.Precision.HIGHEST, preferred_element_type=F32,
    )


def root_curvature(curvature_ref, width):
    rows = lax.broadcasted_iota(jnp.int32, (2, width), 0)
    return jnp.sqrt(jnp.where(rows == 0, curvature_ref[0], curvature_ref[1]))


def first_kernel(curvature_ref, jacobian_ref, index_ref, out_ref, held, sems):
    root = root_curvature(curvature_ref, TILE)
    slot = lax.broadcasted_iota(jnp.int32, (PART, TILE), 0)
    layer = jnp.where(slot < LAYERS, slot, slot - (LAYERS - 1))
    below = (index_ref[...] < layer * SPAN).astype(F32)
    counts = jnp.sum(below, axis=1, keepdims=True)
    eye = lax.broadcasted_iota(jnp.int32, (PART, PART), 0) == lax.broadcasted_iota(jnp.int32, (PART, PART), 1)
    counts = jnp.sum(jnp.where(eye, counts, 0.0), axis=0, keepdims=True)
    high = jnp.floor(counts * (1.0 / 32.0))
    low = counts - 32.0 * high
    rows = lax.broadcasted_iota(jnp.int32, (2, PART), 0)
    tail = jnp.where(rows == 0, high, low).astype(BF16)
    for g in range(GROUPS):
        block = jacobian_ref[:, g * BAND * TILE : g * BAND * TILE + TILE].astype(F32)
        held[g, :, :TILE] = (root * block).astype(BF16)
        held[g, :, TILE:] = tail
    copies = [pltpu.make_async_copy(held, out_ref.at[:, i], sems.at[i]) for i in range(BAND)]
    for copy in copies:
        copy.start()
    for copy in copies:
        copy.wait()


def rest_kernel(curvature_ref, jacobian_ref, out_ref, held, sems):
    root = root_curvature(curvature_ref, REST)
    for g in range(GROUPS):
        block = jacobian_ref[:, g * BAND * TILE + TILE : (g + 1) * BAND * TILE].astype(F32)
        held[g] = (root * block).astype(BF16)
    copies = [pltpu.make_async_copy(held, out_ref.at[:, i], sems.at[i]) for i in range(BAND)]
    for copy in copies:
        copy.start()
    for copy in copies:
        copy.wait()


def factor_part(v_ref):
    sub = lax.broadcasted_iota(jnp.int32, (8, PART), 0)
    steps = PART // 8

    def rows_at(k):
        x = v_ref[8 * k : 8 * k + 8, :]
        return [x[:, :PART], x[:, PART:]]

    def columns(x, k):
        return [jnp.broadcast_to(x[0][:, 8 * k + c : 8 * k + c + 1], (8, PART)) for c in range(8)]

    ahead = {}
    for k in range(steps):
        now = ahead.pop(k) if k in ahead else rows_at(k)
        look = [n for n in (k + 1, k + 2) if n < steps]
        later = {n: (ahead[n] if n in ahead else rows_at(n)) for n in look}
        pivot = columns(now, k)
        below = {n: columns(later[n], k) for n in look}
        scale = jnp.zeros((8, PART), F32)
        for i in range(8):
            value = jnp.broadcast_to(pivot[i][i : i + 1, :], (8, PART))
            inverse = 1.0 / value
            scale = jnp.where(sub == i, value, scale)
            factor = jnp.where(sub > i, pivot[i] * inverse, 0.0)
            factors = {n: below[n][i] * inverse for n in look}
            for c in range(i + 1, 8):
                row = jnp.broadcast_to(pivot[c][i : i + 1, :], (8, PART))
                pivot[c] = pivot[c] - factor * row
                for n in look:
                    below[n][c] = below[n][c] - factors[n] * row
            for h in range(2):
                row = jnp.broadcast_to(now[h][i : i + 1, :], (8, PART))
                now[h] = now[h] - factor * row
                for n in look:
                    later[n][h] = later[n][h] - factors[n] * row
        root = lax.rsqrt(scale)
        done = jnp.concatenate([now[0] * root, now[1] * root], axis=1)
        v_ref[8 * k : 8 * k + 8, :] = done
        ahead.update(later)
        start = 8 * (k + 3)
        if start < PART:
            high, mid, low = thirds(done)
            left = jnp.concatenate([high, high, mid, high, low, mid], axis=0)[:, :PART]
            right = jnp.concatenate([high, mid, high, low, high, mid], axis=0)
            change = dot(left, right, ((0,), (0,)))
            v_ref[start:, :] = v_ref[start:, :] - change[start:, :]


def tile_of(block):
    return block.reshape(EXAMPLES, TILE)


def panel_kernel(lead_ref, first_ref, prior_ref, zt_ref, w_ref, diag_ref, g_ref, v_ref):
    tile = tile_of(first_ref[:, :, :TILE])
    note = first_ref[pl.ds(lead_ref[0], 1), :, TILE:].reshape(2, PART).astype(F32)
    note = 32.0 * note[0:1, :] + note[1:2, :]
    r32 = lax.broadcasted_iota(jnp.int32, (LAYERS, PART), 0)
    c32 = lax.broadcasted_iota(jnp.int32, (LAYERS, PART), 1)
    low = jnp.sum(jnp.where(c32 == r32, note, 0.0), axis=1, keepdims=True)
    high = jnp.sum(jnp.where(c32 == r32 + LAYERS, note, 0.0), axis=1, keepdims=True)
    at = lax.broadcasted_iota(jnp.int32, (LAYERS, TILE), 1).astype(F32)
    inside = (at >= low) & (at < high)
    anchor = jnp.sum(jnp.where(inside, prior_ref[...], 0.0), axis=0, keepdims=True)

    row = lax.broadcasted_iota(jnp.int32, (TILE, TILE), 0)
    column = lax.broadcasted_iota(jnp.int32, (TILE, TILE), 1)
    gram = dot(tile, tile, ((0,), (0,)))
    g_ref[:, :TILE] = jnp.where(row == column, gram + anchor, gram)
    g_ref[:, TILE:] = tile.astype(F32).T
    r128 = lax.broadcasted_iota(jnp.int32, (PART, PART), 0)
    c128 = lax.broadcasted_iota(jnp.int32, (PART, PART), 1)
    eye = (r128 == c128).astype(F32)
    parts = TILE // PART
    for b in range(parts):
        at_rows = slice(b * PART, (b + 1) * PART)
        after = (b + 1) * PART
        v_ref[:, :PART] = g_ref[at_rows, at_rows]
        v_ref[:, PART:] = eye
        factor_part(v_ref)
        diag_ref[at_rows, :] = jnp.where(r128 <= c128, v_ref[:, :PART], 0.0).T
        solved = dot_full(v_ref[:, PART:], g_ref[at_rows, after:], ((1,), (0,)))
        zt_ref[at_rows, :] = solved[:, TILE - after :]
        if b < parts - 1:
            change = dot_full(solved[:, : TILE - after], solved, ((0,), (0,)))
            g_ref[after:, after:] = g_ref[after:, after:] - change
    zt = zt_ref[...]
    r256 = lax.broadcasted_iota(jnp.int32, (EXAMPLES, EXAMPLES), 0)
    c256 = lax.broadcasted_iota(jnp.int32, (EXAMPLES, EXAMPLES), 1)
    w_ref[...] = (r256 == c256).astype(F32) - dot_full(zt, zt, ((0,), (0,)))


def band_kernel(place_ref, first_ref, rest_ref, zt_ref, w_ref, diag_ref, index_ref, prior_ref, out_ref, vh, vl, q_ref):
    place = place_ref[0]
    k = pl.program_id(0)

    @pl.when(k == 0)
    def _():
        def fill(own):
            zh, zl = halves(zt_ref[...])
            q_ref[...] = dot(own, zh, ((0,), (1,))) + dot(own, zl, ((0,), (1,)))

        @pl.when(place == 0)
        def _():
            fill(tile_of(first_ref[:, :, :TILE]))
            q = q_ref[...]
            row = lax.broadcasted_iota(jnp.int32, (TILE, TILE), 0) // PART
            column = lax.broadcasted_iota(jnp.int32, (TILE, TILE), 1) // PART
            diag = jnp.concatenate([diag_ref[...]] * (TILE // PART), axis=1)
            q_ref[...] = jnp.where(row == column, diag, jnp.where(row > column, q, 0.0))

        @pl.when(place > 0)
        def _():
            start = pl.multiple_of((place - 1) * TILE, TILE)
            own = tile_of(rest_ref[:, :, pl.ds(start, TILE)])
            fill(own)
            wh, wl = halves(w_ref[...])
            v = dot(own, wh, ((0,), (0,))) + dot(own, wl, ((0,), (0,)))
            vh[...], vl[...] = halves(v)

    @pl.when(k < place)
    def _():
        start = pl.multiple_of((place - k - 1) * TILE, TILE)
        other = tile_of(rest_ref[:, :, pl.ds(start, TILE)])
        out_ref[0, 0] = dot(vh[...], other, ((1,), (0,))) + dot(vl[...], other, ((1,), (0,)))

    @pl.when((k == 0) & (place > 0))
    def _():
        layer = lax.broadcasted_iota(jnp.int32, (LAYERS, TILE), 0) * SPAN
        index = index_ref[...]
        inside = (index >= layer) & (index < layer + SPAN)
        anchor = jnp.sum(jnp.where(inside, prior_ref[...], 0.0), axis=0, keepdims=True)
        row = lax.broadcasted_iota(jnp.int32, (TILE, TILE), 0)
        column = lax.broadcasted_iota(jnp.int32, (TILE, TILE), 1)
        out_ref[0, 0] = out_ref[0, 0] + jnp.where(row == column, anchor, 0.0)

    @pl.when(k == place)
    def _():
        out_ref[0, 0] = q_ref[...]

    @pl.when(k > place)
    def _():
        out_ref[0, 0] = jnp.zeros((TILE, TILE), F32)


SMEM = pl.BlockSpec(memory_space=pltpu.SMEM)
VMEM = pl.BlockSpec(memory_space=pltpu.VMEM)
HBM = pl.BlockSpec(memory_space=pl.ANY)


def body(jacobian, curvature, sub_index, prior_precision):
    position = lax.axis_index(AXES).astype(jnp.int32)
    index = sub_index.reshape(1, TILE)
    prior = prior_precision.reshape(LAYERS, 1)
    send_first = pl.pallas_call(
        first_kernel,
        out_shape=jax.ShapeDtypeStruct((GROUPS, BAND, 2, WIDE), BF16),
        in_specs=[SMEM, VMEM, VMEM],
        out_specs=HBM,
        scratch_shapes=[pltpu.VMEM((GROUPS, 2, WIDE), BF16), pltpu.SemaphoreType.DMA((BAND,))],
        compiler_params=params(),
        name="first_send",
    )(curvature, jacobian, index)
    first = lax.all_to_all(
        send_first.reshape(DEVICES, 2, WIDE), AXES, split_axis=0, concat_axis=0, tiled=True
    )
    send_rest = pl.pallas_call(
        rest_kernel,
        out_shape=jax.ShapeDtypeStruct((GROUPS, BAND, 2, REST), BF16),
        in_specs=[SMEM, VMEM],
        out_specs=HBM,
        scratch_shapes=[pltpu.VMEM((GROUPS, 2, REST), BF16), pltpu.SemaphoreType.DMA((BAND,))],
        compiler_params=params(),
        name="rest_send",
    )(curvature, jacobian)
    send_rest, first = lax.optimization_barrier((send_rest, first))
    rest = lax.all_to_all(
        send_rest.reshape(DEVICES, 2, REST), AXES, split_axis=0, concat_axis=0, tiled=True
    )
    zt, w, diag = pl.pallas_call(
        panel_kernel,
        out_shape=[
            jax.ShapeDtypeStruct((TILE, EXAMPLES), F32),
            jax.ShapeDtypeStruct((EXAMPLES, EXAMPLES), F32),
            jax.ShapeDtypeStruct((TILE, PART), F32),
        ],
        in_specs=[SMEM, VMEM, VMEM],
        out_specs=[VMEM, VMEM, VMEM],
        scratch_shapes=[pltpu.VMEM((TILE, TILE + EXAMPLES), F32), pltpu.VMEM((PART, 2 * PART), F32)],
        compiler_params=params(),
        cost_estimate=pl.CostEstimate(flops=2 * 10**10, bytes_accessed=2 * 10**6, transcendentals=10**6),
        name="panel",
    )((position // BAND * BAND).reshape(1), first, prior)
    whole = lambda *shape: pl.BlockSpec(shape, lambda k: (0,) * len(shape))
    return pl.pallas_call(
        band_kernel,
        grid=(BAND,),
        out_shape=jax.ShapeDtypeStruct((1, BAND, TILE, TILE), F32),
        in_specs=[
            SMEM,
            whole(DEVICES, 2, WIDE),
            whole(DEVICES, 2, REST),
            whole(TILE, EXAMPLES),
            whole(EXAMPLES, EXAMPLES),
            whole(TILE, PART),
            whole(1, TILE),
            whole(LAYERS, 1),
        ],
        out_specs=pl.BlockSpec((1, 1, TILE, TILE), lambda k: (0, k, 0, 0)),
        scratch_shapes=[
            pltpu.VMEM((TILE, EXAMPLES), BF16),
            pltpu.VMEM((TILE, EXAMPLES), BF16),
            pltpu.VMEM((TILE, TILE), F32),
        ],
        compiler_params=params(),
        name="band",
    )((position % BAND).reshape(1), first, rest, zt, w, diag, index, prior)


def solution(mesh):
    placed = (P(AXES, None), P(AXES), P(AXES), P())
    return jax.shard_map(
        body,
        mesh=mesh,
        in_specs=placed,
        out_specs=P(AXES, None, None, None),
        check_vma=False,
    )
```

time: 476 us -> 65.6 us (0.14); the launches traced: 468 us -> 65.4 us
  other arithmetic: 143 us -> 0 us
  waiting for transfers between devices: 148 us -> 15.5 us
  matrix products: 53.8 us -> 0 us
  local copies, waits for them, and re-layouts: 46.3 us -> 2.65 us
  starting transfers between devices: 51.7 us -> 15.4 us
  Pallas kernels: 0 us -> 31.7 us
  blocking collectives: 20.8 us -> 0 us
    ppermute x14 -> x0, waiting for transfers between devices: 148 us -> none  [shifted(): return lax.ppermute(shard, axis, pairs)]
    another operation x19 -> x0, other arithmetic: 131 us -> none  [the longest x15 79.6 us: body(): factor_tile = jnp.linalg.cholesky(pivot_tile)]
    ppermute x14 -> x0, starting transfers between devices: 51.7 us -> none  [shifted(): return lax.ppermute(shard, axis, pairs)]
    another operation x13 -> x0, matrix products: 37 us -> none  [the longest x7 35.1 us: body(): lax.linalg.triangular_solve(factor_tile, window_slices.reshape(BAND * TIL...]
    pallas_call x0 -> x4, Pallas kernels: none -> 31.7 us  [the longest x1 19.3 us: body(): pl.pallas_call(panel_kernel, out_shape=[jax.ShapeDtypeStruct((TILE, EXAMP...]
    another operation x21 -> x0, local copies, waits for them, and re-layouts: 26.9 us -> none
    all_to_all x1 -> x0, blocking collectives: 20.8 us -> none  [body(): lax.all_to_all(scaled, ('row', 'col'), split_axis=1, concat_axis=0, tiled...]
    dot_general x2 -> x0, matrix products: 16.8 us -> none  [the longest x1 15.5 us: body(): jnp.dot(own_solved, solved.T, precision=lax.Precision.HIGHEST, preferred_...]
  transfers between devices with their start and end apart: 14 -> 2, of which waited for: 10 -> 2; matrix products, arithmetic and copies ran while one was open for 1% -> 1% of each run, Pallas kernels for 0% -> 33%
where the time goes in v1:
time: 65.6 us; the launch traced here: 65.4 us
  Pallas kernels  31.7 us (48%)
  waiting for transfers between devices  15.5 us (24%)
  starting transfers between devices  15.4 us (23%)
  local copies, waits for them, and re-layouts  2.65 us (4%)
    pallas_call x1, Pallas kernels, body(): pl.pallas_call(panel_kernel, out_shape=[jax.ShapeDtypeStruct((TILE, EXAMP...  19.3 us
    all_to_all x1, starting transfers between devices, body(): lax.all_to_all(send_first.reshape(DEVICES, 2, WIDE), AXES, split_axis=0,...  10.5 us
    pallas_call x1, Pallas kernels, body(): pl.pallas_call(band_kernel, grid=(BAND,), out_shape=jax.ShapeDtypeStruct(...  8.05 us
    all_to_all x1, waiting for transfers between devices, body(): lax.all_to_all(send_first.reshape(DEVICES, 2, WIDE), AXES, split_axis=0,...  7.95 us
    all_to_all x1, waiting for transfers between devices, body(): lax.all_to_all(send_rest.reshape(DEVICES, 2, REST), AXES, split_axis=0, c...  7.52 us
    all_to_all x1, starting transfers between devices, body(): lax.all_to_all(send_rest.reshape(DEVICES, 2, REST), AXES, split_axis=0, c...  4.89 us
    pallas_call x1, Pallas kernels, body(): pl.pallas_call(rest_kernel, out_shape=jax.ShapeDtypeStruct((GROUPS, BAND,...  2.49 us
    unnamed x6, local copies, waits for them, and re-layouts  1.97 us
  transfers between devices with their start and end apart: 2, of which 2 were waited for; matrix products, arithmetic and copies ran while one was open for 1% of the time, Pallas kernels for 33%

profile of v1, /device:TPU:2, one launch (start us, length us, event | category | flops | bytes accessed | tf_op | source)
XLA Modules:
  0.0 65.4 jit_solution(11064780646805762630)
XLA Ops:
  0.0 0.0 copy-start.2
  0.0 1.9 %first_send.1 = bf16[16,8,2,640]{3,2,1,0:T(2,128)(2,1)} custom-call(f32[2]{0:T(128)} %curvature_ref.3, bf16[2,65536]{1,0:T(2,128)(2,1)} %jacobian_ref.3, s32[1,512]{1,0:T(1,128)} %bitcast.8), custom_call_target="tpu_custom_call" | custom-call | tf_op jit(solution)/shard_map/first_send/pallas_call | solution.py:244
  1.9 10.5 %all-to-all-start = ((bf16[128,2,640]{2,1,0:T(2,128)(2,1)}), bf16[128,2,640]{2,1,0:T(2,128)(2,1)S(1)}, u32[]{:S(2)}, u32[]{:S(2)}) async-start(bf16[128,2,640]{2,1,0:T(2,128)(2,1)} %bitcast.7), calls=%async_computation | async-start | bytes 655360 | tf_op jit(solution)/shard_map/all_to_all | solution.py:253
  12.5 2.5 %rest_send.1 = bf16[16,8,2,3584]{3,2,1,0:T(2,128)(2,1)} custom-call(f32[2]{0:T(128)} %curvature_ref.3, bf16[2,65536]{1,0:T(2,128)(2,1)} %jacobian_ref.3), custom_call_target="tpu_custom_call" | custom-call | tf_op jit(solution)/shard_map/rest_send/pallas_call | solution.py:256
  15.0 0.0 copy-done.2
  15.0 0.7 %copy.5.prior_ref = f32[32,1]{1,0:T(8,128)} copy(f32[32,1]{0,1:T(1,128)S(1)} %bitcast.10) | data formatting | bytes 256 | tf_op jit(solution)/shard_map/reshape | solution.py:243
  15.7 8.0 %all-to-all-done.first_ref = bf16[128,2,640]{2,1,0:T(2,128)(2,1)S(1)} async-done(((bf16[128,2,640]{2,1,0:T(2,128)(2,1)}), bf16[128,2,640]{2,1,0:T(2,128)(2,1)S(1)}, u32[]{:S(2)}, u32[]{:S(2)}) %all-to-all-start) | async-done | bytes 327712 | tf_op jit(solution)/shard_map/all_to_all | solution.py:253
  23.6 0.0 copy-start.1
  23.6 0.7 %copy-done.1 = bf16[128,2,640]{2,1,0:T(2,128)(2,1)} copy-done((bf16[128,2,640]{2,1,0:T(2,128)(2,1)}, bf16[128,2,640]{2,1,0:T(2,128)(2,1)S(1)}, u32[]{:S(2)}) %copy-start.1) | copy-done | bytes 327704
  24.4 4.9 %all-to-all-start.1 = ((bf16[128,2,3584]{2,1,0:T(2,128)(2,1)}), bf16[128,2,3584]{2,1,0:T(2,128)(2,1)S(1)}, u32[]{:S(2)}, u32[]{:S(2)}) async-start(bf16[128,2,3584]{2,1,0:T(2,128)(2,1)} %bitcast.6), calls=%async_computation.1 | async-start | bytes 3670016 | tf_op jit(solution)/shard_map/all_to_all | solution.py:266
  29.3 19.3 %panel.1 = (f32[512,256]{1,0:T(8,128)}, f32[256,256]{1,0:T(8,128)}, f32[512,128]{1,0:T(8,128)}) custom-call(s32[1]{0:T(128)} %bitcast.4.lead_ref, bf16[128,2,640]{2,1,0:T(2,128)(2,1)} %copy-done.1, f32[32,1]{1,0:T(8,128)} %copy.5.prior_ref), custom_call_target="tpu_custom_call" | custom-call | flops 20000000000 | bytes 2000000 | tf_op jit(solution)/shard_map/panel/pallas_call | solution.py:269
  48.6 7.5 %all-to-all-done.1.rest_ref = bf16[128,2,3584]{2,1,0:T(2,128)(2,1)S(1)} async-done(((bf16[128,2,3584]{2,1,0:T(2,128)(2,1)}), bf16[128,2,3584]{2,1,0:T(2,128)(2,1)S(1)}, u32[]{:S(2)}, u32[]{:S(2)}) %all-to-all-start.1) | async-done | bytes 1835040 | tf_op jit(solution)/shard_map/all_to_all | solution.py:266
  56.1 0.0 copy-start
  56.1 1.2 %copy-done = bf16[128,2,3584]{2,1,0:T(2,128)(2,1)} copy-done((bf16[128,2,3584]{2,1,0:T(2,128)(2,1)}, bf16[128,2,3584]{2,1,0:T(2,128)(2,1)S(1)}, u32[]{:S(2)}) %copy-start) | copy-done | bytes 1835032
  57.3 8.0 %band.1 = f32[1,8,512,512]{3,2,1,0:T(8,128)} custom-call(s32[1]{0:T(128)} %bitcast.place_ref, bf16[128,2,640]{2,1,0:T(2,128)(2,1)} %copy-done.1, bf16[128,2,3584]{2,1,0:T(2,128)(2,1)} %copy-done, f32[512,256]{1,0:T(8,128)} %get-tuple-element.12.zt_ref, f32[256,256]{1,0:T(8,128)} %get-tuple-element.13.w_ref, f32[512,128]{1,0:T(8,128)} %get-tuple-element.14.diag_ref, ...), custom_call_target="tpu_custom_call" | custom-call | tf_op jit(solution)/shard_map/band/pallas_call | solution.py:284
Async XLA Ops:
  0.0 15.0 %copy-start.2 = (f32[32]{0:T(128)S(1)}, f32[32]{0:T(128)}, u32[]{:S(2)}) copy-start(f32[32]{0:T(128)} %param.7) | copy-start | bytes 388
  1.9 21.7 %all-to-all-start = ((bf16[128,2,640]{2,1,0:T(2,128)(2,1)}), bf16[128,2,640]{2,1,0:T(2,128)(2,1)S(1)}, u32[]{:S(2)}, u32[]{:S(2)}) async-start(bf16[128,2,640]{2,1,0:T(2,128)(2,1)} %bitcast.7), calls=%async_computation | async-start | bytes 655360 | tf_op jit(solution)/shard_map/all_to_all | solution.py:253
  23.6 0.7 %copy-start.1 = (bf16[128,2,640]{2,1,0:T(2,128)(2,1)}, bf16[128,2,640]{2,1,0:T(2,128)(2,1)S(1)}, u32[]{:S(2)}) copy-start(bf16[128,2,640]{2,1,0:T(2,128)(2,1)S(1)} %all-to-all-done.first_ref) | copy-start | bytes 983044
  24.4 31.7 %all-to-all-start.1 = ((bf16[128,2,3584]{2,1,0:T(2,128)(2,1)}), bf16[128,2,3584]{2,1,0:T(2,128)(2,1)S(1)}, u32[]{:S(2)}, u32[]{:S(2)}) async-start(bf16[128,2,3584]{2,1,0:T(2,128)(2,1)} %bitcast.6), calls=%async_computation.1 | async-start | bytes 3670016 | tf_op jit(solution)/shard_map/all_to_all | solution.py:266
  56.1 1.2 %copy-start = (bf16[128,2,3584]{2,1,0:T(2,128)(2,1)}, bf16[128,2,3584]{2,1,0:T(2,128)(2,1)S(1)}, u32[]{:S(2)}) copy-start(bf16[128,2,3584]{2,1,0:T(2,128)(2,1)S(1)} %all-to-all-done.1.rest_ref) | copy-start | bytes 5505028

commit v2 on v1

v2 whole, which is shorter than its diff:
```python
import jax
import jax.numpy as jnp
from jax import lax
from jax.experimental import pallas as pl
from jax.experimental.pallas import tpu as pltpu
from jax.sharding import PartitionSpec as P

TILE = 512
BAND = 8
LAYERS = 32
SPAN = 131072
GROUPS = 16
DEVICES = 128
EXAMPLES = 256
WIDE = TILE + 128
REST = (BAND - 2) * TILE
PART = 128
F32 = jnp.float32
BF16 = jnp.bfloat16
AXES = ("row", "col")
VMEM_LIMIT = 56 * 1024 * 1024


def params():
    return pltpu.CompilerParams(vmem_limit_bytes=VMEM_LIMIT)


def halves(x):
    high = x.astype(BF16)
    return high, (x - high.astype(F32)).astype(BF16)


def thirds(x):
    high = x.astype(BF16)
    rest = x - high.astype(F32)
    mid = rest.astype(BF16)
    return high, mid, (rest - mid.astype(F32)).astype(BF16)


def dot(a, b, contract):
    return lax.dot_general(a, b, ((contract[0], contract[1]), ((), ())), preferred_element_type=F32)


def dot_wide(a, b, axis):
    ah, al = halves(a)
    bh, bl = halves(b)
    left = jnp.concatenate([ah, ah, al], axis=axis)
    right = jnp.concatenate([bh, bl, bh], axis=0)
    return dot(left, right, ((axis,), (0,)))


def root_curvature(curvature_ref, width):
    rows = lax.broadcasted_iota(jnp.int32, (2, width), 0)
    return jnp.sqrt(jnp.where(rows == 0, curvature_ref[0], curvature_ref[1]))


def first_kernel(curvature_ref, jacobian_ref, index_ref, out_ref, shared, own, sems):
    root = root_curvature(curvature_ref, BAND * TILE)
    slot = lax.broadcasted_iota(jnp.int32, (PART, TILE), 0)
    layer = jnp.where(slot < LAYERS, slot, slot - (LAYERS - 1))
    below = (index_ref[...] < layer * SPAN).astype(F32)
    counts = jnp.sum(below, axis=1, keepdims=True)
    eye = lax.broadcasted_iota(jnp.int32, (PART, PART), 0) == lax.broadcasted_iota(jnp.int32, (PART, PART), 1)
    counts = jnp.sum(jnp.where(eye, counts, 0.0), axis=0, keepdims=True)
    high = jnp.floor(counts * (1.0 / 32.0))
    low = counts - 32.0 * high
    rows = lax.broadcasted_iota(jnp.int32, (2, PART), 0)
    tail = jnp.where(rows == 0, high, low).astype(BF16)
    for g in range(GROUPS):
        block = jacobian_ref[:, g * BAND * TILE : (g + 1) * BAND * TILE].astype(F32)
        block = (root * block).astype(BF16)
        shared[g, :, :TILE] = block[:, :TILE]
        shared[g, :, TILE:] = tail
        for i in range(BAND):
            own[g, i] = block[:, i * TILE : (i + 1) * TILE]
    copies = [
        pltpu.make_async_copy(shared, out_ref.at[:, i, :, pl.ds(0, WIDE)], sems.at[i])
        for i in range(BAND)
    ]
    copies.append(pltpu.make_async_copy(own, out_ref.at[:, :, :, pl.ds(WIDE, TILE)], sems.at[BAND]))
    for copy in copies:
        copy.start()
    for copy in copies:
        copy.wait()


def rest_kernel(curvature_ref, jacobian_ref, out_ref, held, sems):
    root = root_curvature(curvature_ref, REST)
    for g in range(GROUPS):
        start = g * BAND * TILE + TILE
        block = jacobian_ref[:, start : start + REST].astype(F32)
        held[g] = (root * block).astype(BF16)
    copies = [pltpu.make_async_copy(held, out_ref.at[:, i], sems.at[i]) for i in range(BAND)]
    for copy in copies:
        copy.start()
    for copy in copies:
        copy.wait()


def factor_part(v_ref, d_ref):
    sub = lax.broadcasted_iota(jnp.int32, (8, PART), 0)
    lane = lax.broadcasted_iota(jnp.int32, (8, PART), 1)
    steps = PART // 8

    def spread(x):
        return jnp.broadcast_to(x, (8, PART))

    def rows_at(k):
        return v_ref[8 * k : 8 * k + 8, :]

    def columns(x, k):
        return [spread(x[:, 8 * k + c : 8 * k + c + 1]) for c in range(8)]

    held = {k: rows_at(k) for k in range(3)}
    pivot = columns(held[0], 0)
    near = columns(held[1], 0)
    for k in range(steps):
        now, one, two = held.pop(k), held.get(k + 1), held.get(k + 2)
        far = columns(two, k) if two is not None else None
        next_pivot = columns(one, k + 1) if one is not None else None
        next_near = columns(two, k + 1) if two is not None else None
        here = (lane >= 8 * k) & (lane < 8 * k + 8)
        now = jnp.where(here, (lane - 8 * k == sub).astype(F32), now)
        if one is not None:
            one = jnp.where(here, 0.0, one)
        if two is not None:
            two = jnp.where(here, 0.0, two)
        scale = jnp.zeros((8, PART), F32)
        for i in range(8):
            value = spread(pivot[i][i : i + 1])
            inverse = 1.0 / value
            scale = jnp.where(sub == i, value, scale)
            f0 = jnp.where(sub > i, pivot[i] * inverse, 0.0)
            f1 = near[i] * inverse if one is not None else None
            f2 = far[i] * inverse if two is not None else None
            for c in range(i + 1, 8):
                row = spread(pivot[c][i : i + 1])
                pivot[c] = pivot[c] - f0 * row
                if one is not None:
                    near[c] = near[c] - f1 * row
                if two is not None:
                    far[c] = far[c] - f2 * row
            if one is not None:
                for c in range(8):
                    row = spread(near[i][c : c + 1])
                    next_pivot[c] = next_pivot[c] - f1 * row
                    if two is not None:
                        next_near[c] = next_near[c] - f2 * row
            row = spread(now[i : i + 1])
            now = now - f0 * row
            if one is not None:
                one = one - f1 * row
            if two is not None:
                two = two - f2 * row
        root = lax.rsqrt(scale)
        done = now * root
        v_ref[8 * k : 8 * k + 8, :] = done
        block = jnp.zeros((8, PART), F32)
        for c in range(8):
            block = jnp.where((lane == 8 * k + c) & (sub <= c), pivot[c], block)
        d_ref[8 * k : 8 * k + 8, :] = block * root
        if one is not None:
            held[k + 1] = one
        if two is not None:
            held[k + 2] = two
        pivot, near = next_pivot, next_near
        start = 8 * (k + 3)
        if start < PART:
            high, mid, low = thirds(done)
            left = jnp.concatenate([high, high, mid, high, low, mid], axis=0)
            right = jnp.concatenate([high, mid, high, low, high, mid], axis=0)
            change = dot(left, right, ((0,), (0,)))
            at = lax.broadcasted_iota(jnp.int32, (PART - start, PART), 1)
            keep = jnp.where((at >= 8 * k) & (at < 8 * k + 8), 0.0, v_ref[start:, :])
            v_ref[start:, :] = keep - change[start:, :]
            held[k + 3] = rows_at(k + 3)


def tile_of(block):
    return block.reshape(EXAMPLES, TILE)


def layer_anchor(low, high, at, prior_ref):
    inside = (at >= low) & (at < high)
    return jnp.sum(jnp.where(inside, prior_ref[...], 0.0), axis=0, keepdims=True)


def panel_kernel(info_ref, first_ref, index_ref, prior_ref, out_ref, v_ref, *scratch):
    parts = TILE // PART
    r_refs, (t_ref, f_ref, d_ref, made, zero, sems) = scratch[:parts], scratch[parts:]
    lead, place = info_ref[0], info_ref[1]

    def store(source, k):
        return pltpu.make_async_copy(source, out_ref.at[0, k], sems.at[k])

    zero[...] = jnp.zeros((TILE, TILE), F32)
    for k in range(1, BAND):
        @pl.when(k > place)
        def _():
            store(zero, k).start()

    tile = tile_of(first_ref[:, :, :TILE])
    own = tile_of(first_ref[:, :, WIDE:])
    own2 = jnp.concatenate([own, own], axis=0)
    note = first_ref[pl.ds(lead, 1), :, TILE:WIDE].reshape(2, PART).astype(F32)
    note = 32.0 * note[0:1, :] + note[1:2, :]
    r32 = lax.broadcasted_iota(jnp.int32, (LAYERS, PART), 0)
    c32 = lax.broadcasted_iota(jnp.int32, (LAYERS, PART), 1)
    low = jnp.sum(jnp.where(c32 == r32, note, 0.0), axis=1, keepdims=True)
    high = jnp.sum(jnp.where(c32 == r32 + LAYERS, note, 0.0), axis=1, keepdims=True)
    at = lax.broadcasted_iota(jnp.int32, (LAYERS, TILE), 1).astype(F32)
    anchor = layer_anchor(low, high, at, prior_ref)

    r128 = lax.broadcasted_iota(jnp.int32, (PART, PART), 0)
    c128 = lax.broadcasted_iota(jnp.int32, (PART, PART), 1)
    turned = tile.astype(F32).T
    for b in range(parts):
        block = slice(b * PART, (b + 1) * PART)
        gram = dot(tile[:, block], tile[:, b * PART :], ((0,), (0,)))
        t_ref[b] = gram[:, :PART] + jnp.where(r128 == c128, anchor[:, block], 0.0)
        if b < parts - 1:
            r_refs[b][:, : TILE - (b + 1) * PART] = gram[:, PART:]
        r_refs[b][:, TILE - (b + 1) * PART :] = turned[block, :]

    r256 = lax.broadcasted_iota(jnp.int32, (EXAMPLES, EXAMPLES), 0)
    c256 = lax.broadcasted_iota(jnp.int32, (EXAMPLES, EXAMPLES), 1)
    w = (r256 == c256).astype(F32)
    for b in range(parts):
        block = slice(b * PART, (b + 1) * PART)
        after = (b + 1) * PART
        f_ref[b] = t_ref[b]
        factor_part(f_ref.at[b], d_ref.at[b])
        f = f_ref[b]
        inverse = jnp.where(c128 // 8 <= r128 // 8, f, 0.0)
        d_ref[b] = jnp.where(c128 // 8 > r128 // 8, f, d_ref[b])
        if b < parts - 1:
            first = dot_wide(inverse, r_refs[b][:, :PART], 1)
            t_ref[b + 1] = t_ref[b + 1] - dot_wide(first, first, 0)
            others = dot_wide(inverse, r_refs[b][:, PART:], 1)
            solved = jnp.concatenate([first, others], axis=1)
            for c in range(b + 1, parts):
                skip = (c - b - 1) * PART
                change = dot_wide(solved[:, skip : skip + PART], solved[:, skip:], 0)
                if c > b + 1:
                    t_ref[c] = t_ref[c] - change[:, :PART]
                r_refs[c][...] = r_refs[c][...] - change[:, PART:]
        else:
            solved = dot_wide(inverse, r_refs[b][...], 1)
        zt = solved[:, TILE - after :]
        z2 = jnp.concatenate(halves(zt), axis=1)
        made[1, :, block] = dot(own2, z2, ((0,), (1,)))
        w = w - dot_wide(zt, zt, 0)

    @pl.when(place == 0)
    def _():
        for b in range(parts):
            block = slice(b * PART, (b + 1) * PART)
            if b > 0:
                made[1, : b * PART, block] = jnp.zeros((b * PART, PART), F32)
            made[1, block, block] = d_ref[b].T

    store(made.at[1], place).start()
    w2 = jnp.concatenate(halves(w), axis=0)
    v = jnp.concatenate(halves(dot(own2, w2, ((0,), (0,)))), axis=1)
    v_ref[...] = v

    @pl.when(place > 0)
    def _():
        layer = lax.broadcasted_iota(jnp.int32, (LAYERS, TILE), 0) * SPAN
        own_anchor = layer_anchor(layer, layer + SPAN, index_ref[...], prior_ref)
        row = lax.broadcasted_iota(jnp.int32, (TILE, TILE), 0)
        column = lax.broadcasted_iota(jnp.int32, (TILE, TILE), 1)
        made[0] = dot(v_ref[...], own2, ((1,), (0,))) + jnp.where(row == column, own_anchor, 0.0)
        store(made.at[0], 0).start()
        store(made.at[0], 0).wait()

    store(made.at[1], place).wait()
    for k in range(1, BAND):
        @pl.when(k > place)
        def _():
            store(zero, k).wait()


def band_kernel(place_ref, v_ref, rest_ref, before_ref, out_ref, made, sems):
    place = place_ref[0]

    def store(k):
        return pltpu.make_async_copy(made.at[k - 1], out_ref.at[0, k], sems.at[k - 1])

    for k in range(1, BAND - 1):
        @pl.when(k < place)
        def _():
            start = pl.multiple_of((place - k - 1) * TILE, TILE)
            other = tile_of(rest_ref[:, :, pl.ds(start, TILE)])
            made[k - 1] = dot(v_ref[...], jnp.concatenate([other, other], axis=0), ((1,), (0,)))
            store(k).start()

    for k in range(1, BAND - 1):
        @pl.when(k < place)
        def _():
            store(k).wait()


SMEM = pl.BlockSpec(memory_space=pltpu.SMEM)
VMEM = pl.BlockSpec(memory_space=pltpu.VMEM)
HBM = pl.BlockSpec(memory_space=pl.ANY)


def body(jacobian, curvature, sub_index, prior_precision):
    position = lax.axis_index(AXES).astype(jnp.int32)
    place = lax.rem(position, BAND)
    index = sub_index.reshape(1, TILE)
    prior = prior_precision.reshape(LAYERS, 1)
    send_first = pl.pallas_call(
        first_kernel,
        out_shape=jax.ShapeDtypeStruct((GROUPS, BAND, 2, WIDE + TILE), BF16),
        in_specs=[SMEM, VMEM, VMEM],
        out_specs=HBM,
        scratch_shapes=[
            pltpu.VMEM((GROUPS, 2, WIDE), BF16),
            pltpu.VMEM((GROUPS, BAND, 2, TILE), BF16),
            pltpu.SemaphoreType.DMA((BAND + 1,)),
        ],
        compiler_params=params(),
        name="first_send",
    )(curvature, jacobian, index)
    first = lax.all_to_all(
        send_first.reshape(DEVICES, 2, WIDE + TILE), AXES, split_axis=0, concat_axis=0, tiled=True
    )
    send_rest = pl.pallas_call(
        rest_kernel,
        out_shape=jax.ShapeDtypeStruct((GROUPS, BAND, 2, REST), BF16),
        in_specs=[SMEM, VMEM],
        out_specs=HBM,
        scratch_shapes=[pltpu.VMEM((GROUPS, 2, REST), BF16), pltpu.SemaphoreType.DMA((BAND,))],
        compiler_params=params(),
        name="rest_send",
    )(curvature, jacobian)
    send_rest, first = lax.optimization_barrier((send_rest, first))
    rest = lax.all_to_all(
        send_rest.reshape(DEVICES, 2, REST), AXES, split_axis=0, concat_axis=0, tiled=True
    )
    parts = TILE // PART
    before, v = pl.pallas_call(
        panel_kernel,
        out_shape=[
            jax.ShapeDtypeStruct((1, BAND, TILE, TILE), F32),
            jax.ShapeDtypeStruct((TILE, 2 * EXAMPLES), BF16),
        ],
        in_specs=[SMEM, VMEM, VMEM, VMEM],
        out_specs=[HBM, VMEM],
        scratch_shapes=[pltpu.VMEM((PART, TILE - (b + 1) * PART + EXAMPLES), F32) for b in range(parts)]
        + [
            pltpu.VMEM((parts, PART, PART), F32),
            pltpu.VMEM((parts, PART, PART), F32),
            pltpu.VMEM((parts, PART, PART), F32),
            pltpu.VMEM((2, TILE, TILE), F32),
            pltpu.VMEM((TILE, TILE), F32),
            pltpu.SemaphoreType.DMA((BAND,)),
        ],
        compiler_params=params(),
        cost_estimate=pl.CostEstimate(flops=2 * 10**10, bytes_accessed=2 * 10**6, transcendentals=10**6),
        name="panel",
    )(jnp.stack([position - place, place]), pltpu.with_memory_space_constraint(first, pltpu.VMEM), index, prior)
    return pl.pallas_call(
        band_kernel,
        out_shape=jax.ShapeDtypeStruct((1, BAND, TILE, TILE), F32),
        in_specs=[SMEM, VMEM, VMEM, HBM],
        out_specs=HBM,
        scratch_shapes=[
            pltpu.VMEM((BAND - 2, TILE, TILE), F32),
            pltpu.SemaphoreType.DMA((BAND - 2,)),
        ],
        input_output_aliases={3: 0},
        compiler_params=params(),
        name="band",
    )(place.reshape(1), v, pltpu.with_memory_space_constraint(rest, pltpu.VMEM), before)


def solution(mesh):
    placed = (P(AXES, None), P(AXES), P(AXES), P())
    return jax.shard_map(
        body,
        mesh=mesh,
        in_specs=placed,
        out_specs=P(AXES, None, None, None),
        check_vma=False,
    )
```

time: 65.6 us -> 59.4 us (0.905)
  Pallas kernels: 31.7 us -> 24.7 us
  waiting for transfers between devices: 15.5 us -> 16.9 us
  local copies, waits for them, and re-layouts: 2.65 us -> 1.33 us
    pallas_call x2, Pallas kernels: 27.3 us -> 20.2 us  [the longest x1 16.8 us: body(): pl.pallas_call(panel_kernel, out_shape=[jax.ShapeDtypeStruct((1, BAND, TI...]
    unnamed x6 -> x0, local copies, waits for them, and re-layouts: 1.97 us -> none
    all_to_all x1, waiting for transfers between devices: 7.95 us -> 9.47 us  [body(): lax.all_to_all(send_first.reshape(DEVICES, 2, WIDE + TILE), AXES, split_a...]
  transfers between devices with their start and end apart: 2 -> 2, of which waited for: 2 -> 2; matrix products, arithmetic and copies ran while one was open for 1% -> 3% of each run, Pallas kernels for 33% -> 33%
where the time goes in v2:
time: 59.4 us; the launch traced here: 59 us
  Pallas kernels  24.7 us (42%)
  waiting for transfers between devices  16.9 us (28%)
  starting transfers between devices  15.4 us (26%)
  local copies, waits for them, and re-layouts  1.33 us (2%)
  other arithmetic  0.65 us (1%)
    pallas_call x1, Pallas kernels, body(): pl.pallas_call(panel_kernel, out_shape=[jax.ShapeDtypeStruct((1, BAND, TI...  16.8 us
    all_to_all x1, starting transfers between devices, body(): lax.all_to_all(send_first.reshape(DEVICES, 2, WIDE + TILE), AXES, split_a...  10.5 us
    all_to_all x1, waiting for transfers between devices, body(): lax.all_to_all(send_first.reshape(DEVICES, 2, WIDE + TILE), AXES, split_a...  9.47 us
    all_to_all x1, waiting for transfers between devices, body(): lax.all_to_all(send_rest.reshape(DEVICES, 2, REST), AXES, split_axis=0, c...  7.39 us
    all_to_all x1, starting transfers between devices, body(): lax.all_to_all(send_rest.reshape(DEVICES, 2, REST), AXES, split_axis=0, c...  4.89 us
    pallas_call x1, Pallas kernels, body(): pl.pallas_call(band_kernel, out_shape=jax.ShapeDtypeStruct((1, BAND, TILE...  3.41 us
    pallas_call x1, Pallas kernels, body(): pl.pallas_call(rest_kernel, out_shape=jax.ShapeDtypeStruct((GROUPS, BAND,...  2.43 us
    pallas_call x1, Pallas kernels, body(): pl.pallas_call(first_kernel, out_shape=jax.ShapeDtypeStruct((GROUPS, BAND...  2.05 us
  transfers between devices with their start and end apart: 2, of which 2 were waited for; matrix products, arithmetic and copies ran while one was open for 3% of the time, Pallas kernels for 33%

profile of v2, /device:TPU:2, one launch (start us, length us, event | category | flops | bytes accessed | tf_op | source)
XLA Modules:
  0.0 59.0 jit_solution(13405816657605476592)
XLA Ops:
  0.0 2.0 %first_send.1 = bf16[16,8,2,1152]{3,2,1,0:T(2,128)(2,1)} custom-call(f32[2]{0:T(128)} %curvature_ref.3, bf16[2,65536]{1,0:T(2,128)(2,1)} %jacobian_ref.3, s32[1,512]{1,0:T(1,128)} %bitcast.8), custom_call_target="tpu_custom_call" | custom-call | tf_op jit(solution)/shard_map/first_send/pallas_call | solution.py:314
  2.1 10.5 %all-to-all-start = ((bf16[128,2,1152]{2,1,0:T(2,128)(2,1)}), bf16[128,2,1152]{2,1,0:T(2,128)(2,1)S(1)}, u32[]{:S(2)}, u32[]{:S(2)}) async-start(bf16[128,2,1152]{2,1,0:T(2,128)(2,1)} %bitcast.7), calls=%async_computation | async-start | bytes 1179648 | tf_op jit(solution)/shard_map/all_to_all | solution.py:327
  12.6 2.4 %rest_send.1 = bf16[16,8,2,3072]{3,2,1,0:T(2,128)(2,1)} custom-call(f32[2]{0:T(128)} %curvature_ref.3, bf16[2,65536]{1,0:T(2,128)(2,1)} %jacobian_ref.3), custom_call_target="tpu_custom_call" | custom-call | tf_op jit(solution)/shard_map/rest_send/pallas_call | solution.py:330
  15.0 1.3 %copy.6.prior_ref = f32[32,1]{1,0:T(8,128)} copy(f32[32,1]{0,1:T(1,128)} %bitcast.10) | data formatting | bytes 256 | tf_op jit(solution)/shard_map/reshape | solution.py:313
  16.4 0.7 %pad_add_fusion.info_ref = s32[2]{0:T(128)} fusion(s32[1]{0:T(128)} %bitcast.place_ref, s32[1]{0:T(128)} %bitcast.1), kind=kLoop, calls=%fused_computation | loop fusion | flops 2 | bytes 16 | tf_op jit(solution)/shard_map/stack | solution.py:364
  17.0 9.5 %all-to-all-done.first_ref = bf16[128,2,1152]{2,1,0:T(2,128)(2,1)S(1)} async-done(((bf16[128,2,1152]{2,1,0:T(2,128)(2,1)}), bf16[128,2,1152]{2,1,0:T(2,128)(2,1)S(1)}, u32[]{:S(2)}, u32[]{:S(2)}) %all-to-all-start) | async-done | bytes 589856 | tf_op jit(solution)/shard_map/all_to_all | solution.py:327
  26.5 4.9 %all-to-all-start.1 = ((bf16[128,2,3072]{2,1,0:T(2,128)(2,1)}), bf16[128,2,3072]{2,1,0:T(2,128)(2,1)S(1)}, u32[]{:S(2)}, u32[]{:S(2)}) async-start(bf16[128,2,3072]{2,1,0:T(2,128)(2,1)} %bitcast.6), calls=%async_computation.1 | async-start | bytes 3145728 | tf_op jit(solution)/shard_map/all_to_all | solution.py:340
  31.4 16.8 %panel.1 = (f32[1,8,512,512]{3,2,1,0:T(8,128)}, bf16[512,512]{1,0:T(8,128)(2,1)}) custom-call(s32[2]{0:T(128)} %pad_add_fusion.info_ref, bf16[128,2,1152]{2,1,0:T(2,128)(2,1)S(1)} %all-to-all-done.first_ref, s32[1,512]{1,0:T(1,128)} %bitcast.9, f32[32,1]{1,0:T(8,128)} %copy.6.prior_ref), custom_call_target="tpu_custom_call" | custom-call | flops 20000000000 | bytes 2000000 | tf_op jit(solution)/shard_map/panel/pallas_call | solution.py:344
  48.2 7.4 %all-to-all-done.1.rest_ref = bf16[128,2,3072]{2,1,0:T(2,128)(2,1)S(1)} async-done(((bf16[128,2,3072]{2,1,0:T(2,128)(2,1)}), bf16[128,2,3072]{2,1,0:T(2,128)(2,1)S(1)}, u32[]{:S(2)}, u32[]{:S(2)}) %all-to-all-start.1) | async-done | bytes 1572896 | tf_op jit(solution)/shard_map/all_to_all | solution.py:340
  55.6 3.4 %band.1 = f32[1,8,512,512]{3,2,1,0:T(8,128)} custom-call(s32[1]{0:T(128)} %bitcast.place_ref, bf16[512,512]{1,0:T(8,128)(2,1)} %get-tuple-element.10.v_ref, bf16[128,2,3072]{2,1,0:T(2,128)(2,1)S(1)} %all-to-all-done.1.rest_ref, f32[1,8,512,512]{3,2,1,0:T(8,128)} %get-tuple-element.12.before_ref), custom_call_target="tpu_custom_call", output_to_operand_aliasing={{}: (3, {})} | custom-call | tf_op jit(solution)/shard_map/band/pallas_call | solution.py:365
Async XLA Ops:
  2.1 24.4 %all-to-all-start = ((bf16[128,2,1152]{2,1,0:T(2,128)(2,1)}), bf16[128,2,1152]{2,1,0:T(2,128)(2,1)S(1)}, u32[]{:S(2)}, u32[]{:S(2)}) async-start(bf16[128,2,1152]{2,1,0:T(2,128)(2,1)} %bitcast.7), calls=%async_computation | async-start | bytes 1179648 | tf_op jit(solution)/shard_map/all_to_all | solution.py:327
  26.5 29.1 %all-to-all-start.1 = ((bf16[128,2,3072]{2,1,0:T(2,128)(2,1)}), bf16[128,2,3072]{2,1,0:T(2,128)(2,1)S(1)}, u32[]{:S(2)}, u32[]{:S(2)}) async-start(bf16[128,2,3072]{2,1,0:T(2,128)(2,1)} %bitcast.6), calls=%async_computation.1 | async-start | bytes 3145728 | tf_op jit(solution)/shard_map/all_to_all | solution.py:340

commit v3 on v2

--- a/solution.py
+++ b/solution.py
@@ -13,7 +13,7 @@
 DEVICES = 128
 EXAMPLES = 256
 WIDE = TILE + 128
-REST = (BAND - 2) * TILE
+REST = (BAND - 3) * TILE
 PART = 128
 F32 = jnp.float32
 BF16 = jnp.bfloat16
@@ -28,13 +28,6 @@
 def halves(x):
     high = x.astype(BF16)
     return high, (x - high.astype(F32)).astype(BF16)
-
-
-def thirds(x):
-    high = x.astype(BF16)
-    rest = x - high.astype(F32)
-    mid = rest.astype(BF16)
-    return high, mid, (rest - mid.astype(F32)).astype(BF16)
 
 
 def dot(a, b, contract):
@@ -54,7 +47,7 @@
     return jnp.sqrt(jnp.where(rows == 0, curvature_ref[0], curvature_ref[1]))
 
 
-def first_kernel(curvature_ref, jacobian_ref, index_ref, out_ref, shared, own, sems):
+def first_kernel(curvature_ref, jacobian_ref, index_ref, out_ref):
     root = root_curvature(curvature_ref, BAND * TILE)
     slot = lax.broadcasted_iota(jnp.int32, (PART, TILE), 0)
     layer = jnp.where(slot < LAYERS, slot, slot - (LAYERS - 1))
@@ -69,19 +62,10 @@
     for g in range(GROUPS):
         block = jacobian_ref[:, g * BAND * TILE : (g + 1) * BAND * TILE].astype(F32)
         block = (root * block).astype(BF16)
-        shared[g, :, :TILE] = block[:, :TILE]
-        shared[g, :, TILE:] = tail
         for i in range(BAND):
-            own[g, i] = block[:, i * TILE : (i + 1) * TILE]
-    copies = [
-        pltpu.make_async_copy(shared, out_ref.at[:, i, :, pl.ds(0, WIDE)], sems.at[i])
-        for i in range(BAND)
-    ]
-    copies.append(pltpu.make_async_copy(own, out_ref.at[:, :, :, pl.ds(WIDE, TILE)], sems.at[BAND]))
-    for copy in copies:
-        copy.start()
-    for copy in copies:
-        copy.wait()
+            out_ref[g, i, :, :TILE] = block[:, :TILE]
+            out_ref[g, i, :, TILE:WIDE] = tail
+            out_ref[g, i, :, WIDE:] = block[:, i * TILE : (i + 1) * TILE]
 
 
 def rest_kernel(curvature_ref, jacobian_ref, out_ref, held, sems):
@@ -97,7 +81,7 @@
         copy.wait()
 
 
-def factor_part(v_ref, d_ref):
+def factor_part(v_ref):
     sub = lax.broadcasted_iota(jnp.int32, (8, PART), 0)
     lane = lax.broadcasted_iota(jnp.int32, (8, PART), 1)
     steps = PART // 8
@@ -116,6 +100,13 @@
     near = columns(held[1], 0)
     for k in range(steps):
         now, one, two = held.pop(k), held.get(k + 1), held.get(k + 2)
+        start = 8 * (k + 3)
+        if start < PART:
+            below = v_ref[start:, :]
+            high, low = halves(below)
+            left = jnp.concatenate([high, high, low], axis=1)
+            at = lax.broadcasted_iota(jnp.int32, (PART - start, PART), 1)
+            keep = jnp.where((at >= 8 * k) & (at < 8 * k + 8), 0.0, below)
         far = columns(two, k) if two is not None else None
         next_pivot = columns(one, k + 1) if one is not None else None
         next_near = columns(two, k + 1) if two is not None else None
@@ -126,11 +117,16 @@
         if two is not None:
             two = jnp.where(here, 0.0, two)
         scale = jnp.zeros((8, PART), F32)
+        unscale = scale
+        done = now
         for i in range(8):
             value = spread(pivot[i][i : i + 1])
             inverse = 1.0 / value
             scale = jnp.where(sub == i, value, scale)
-            f0 = jnp.where(sub > i, pivot[i] * inverse, 0.0)
+            unscale = jnp.where(sub == i, inverse, unscale)
+            if i > 0:
+                done = jnp.where(sub == i, now, done)
+            f0 = jnp.where(sub != i, pivot[i] * inverse, 0.0)
             f1 = near[i] * inverse if one is not None else None
             f2 = far[i] * inverse if two is not None else None
             for c in range(i + 1, 8):
@@ -152,27 +148,19 @@
                 one = one - f1 * row
             if two is not None:
                 two = two - f2 * row
-        root = lax.rsqrt(scale)
-        done = now * root
-        v_ref[8 * k : 8 * k + 8, :] = done
-        block = jnp.zeros((8, PART), F32)
-        for c in range(8):
-            block = jnp.where((lane == 8 * k + c) & (sub <= c), pivot[c], block)
-        d_ref[8 * k : 8 * k + 8, :] = block * root
+        v_ref[8 * k : 8 * k + 8, :] = done * lax.rsqrt(scale)
         if one is not None:
             held[k + 1] = one
         if two is not None:
             held[k + 2] = two
         pivot, near = next_pivot, next_near
-        start = 8 * (k + 3)
         if start < PART:
-            high, mid, low = thirds(done)
-            left = jnp.concatenate([high, high, mid, high, low, mid], axis=0)
-            right = jnp.concatenate([high, mid, high, low, high, mid], axis=0)
-            change = dot(left, right, ((0,), (0,)))
-            at = lax.broadcasted_iota(jnp.int32, (PART - start, PART), 1)
-            keep = jnp.where((at >= 8 * k) & (at < 8 * k + 8), 0.0, v_ref[start:, :])
-            v_ref[start:, :] = keep - change[start:, :]
+            rows = [now * unscale, jnp.zeros((PART - 8 - 8 * k, PART), F32)]
+            if k > 0:
+                rows = [jnp.zeros((8 * k, PART), F32)] + rows
+            high, low = halves(jnp.concatenate(rows, axis=0))
+            right = jnp.concatenate([high, low, high], axis=0)
+            v_ref[start:, :] = keep - dot(left, right, ((1,), (0,)))
             held[k + 3] = rows_at(k + 3)
 
 
@@ -187,7 +175,7 @@
 
 def panel_kernel(info_ref, first_ref, index_ref, prior_ref, out_ref, v_ref, *scratch):
     parts = TILE // PART
-    r_refs, (t_ref, f_ref, d_ref, made, zero, sems) = scratch[:parts], scratch[parts:]
+    r_refs, (t_ref, f_ref, z_ref, made, zero, sems) = scratch[:parts], scratch[parts:]
     lead, place = info_ref[0], info_ref[1]
 
     def store(source, k):
@@ -201,7 +189,8 @@
 
     tile = tile_of(first_ref[:, :, :TILE])
     own = tile_of(first_ref[:, :, WIDE:])
-    own2 = jnp.concatenate([own, own], axis=0)
+    turned_own = own.T
+    own2 = jnp.concatenate([turned_own, turned_own], axis=1)
     note = first_ref[pl.ds(lead, 1), :, TILE:WIDE].reshape(2, PART).astype(F32)
     note = 32.0 * note[0:1, :] + note[1:2, :]
     r32 = lax.broadcasted_iota(jnp.int32, (LAYERS, PART), 0)
@@ -222,17 +211,12 @@
             r_refs[b][:, : TILE - (b + 1) * PART] = gram[:, PART:]
         r_refs[b][:, TILE - (b + 1) * PART :] = turned[block, :]
 
-    r256 = lax.broadcasted_iota(jnp.int32, (EXAMPLES, EXAMPLES), 0)
-    c256 = lax.broadcasted_iota(jnp.int32, (EXAMPLES, EXAMPLES), 1)
-    w = (r256 == c256).astype(F32)
     for b in range(parts):
         block = slice(b * PART, (b + 1) * PART)
         after = (b + 1) * PART
         f_ref[b] = t_ref[b]
-        factor_part(f_ref.at[b], d_ref.at[b])
-        f = f_ref[b]
-        inverse = jnp.where(c128 // 8 <= r128 // 8, f, 0.0)
-        d_ref[b] = jnp.where(c128 // 8 > r128 // 8, f, d_ref[b])
+        factor_part(f_ref.at[b])
+        inverse = jnp.where(c128 <= r128, f_ref[b], 0.0)
         if b < parts - 1:
             first = dot_wide(inverse, r_refs[b][:, :PART], 1)
             t_ref[b + 1] = t_ref[b + 1] - dot_wide(first, first, 0)
@@ -247,9 +231,10 @@
         else:
             solved = dot_wide(inverse, r_refs[b][...], 1)
         zt = solved[:, TILE - after :]
-        z2 = jnp.concatenate(halves(zt), axis=1)
-        made[1, :, block] = dot(own2, z2, ((0,), (1,)))
-        w = w - dot_wide(zt, zt, 0)
+        z_ref[block, :] = zt
+
+    zt = z_ref[...]
+    made[1] = dot(own2, jnp.concatenate(halves(zt), axis=1), ((1,), (1,)))
 
     @pl.when(place == 0)
     def _():
@@ -257,11 +242,19 @@
             block = slice(b * PART, (b + 1) * PART)
             if b > 0:
                 made[1, : b * PART, block] = jnp.zeros((b * PART, PART), F32)
-            made[1, block, block] = d_ref[b].T
+            inverse = jnp.where(c128 <= r128, f_ref[b], 0.0)
+            th, tl = halves(t_ref[b])
+            ih, il = halves(inverse)
+            left = jnp.concatenate([th, th, tl], axis=1)
+            right = jnp.concatenate([ih, il, ih], axis=1)
+            made[1, block, block] = jnp.where(c128 <= r128, dot(left, right, ((1,), (1,))), 0.0)
 
     store(made.at[1], place).start()
+    r256 = lax.broadcasted_iota(jnp.int32, (EXAMPLES, EXAMPLES), 0)
+    c256 = lax.broadcasted_iota(jnp.int32, (EXAMPLES, EXAMPLES), 1)
+    w = (r256 == c256).astype(F32) - dot_wide(zt, zt, 0)
     w2 = jnp.concatenate(halves(w), axis=0)
-    v = jnp.concatenate(halves(dot(own2, w2, ((0,), (0,)))), axis=1)
+    v = jnp.concatenate(halves(dot(own2, w2, ((1,), (0,)))), axis=1)
     v_ref[...] = v
 
     @pl.when(place > 0)
@@ -270,7 +263,9 @@
         own_anchor = layer_anchor(layer, layer + SPAN, index_ref[...], prior_ref)
         row = lax.broadcasted_iota(jnp.int32, (TILE, TILE), 0)
         column = lax.broadcasted_iota(jnp.int32, (TILE, TILE), 1)
-        made[0] = dot(v_ref[...], own2, ((1,), (0,))) + jnp.where(row == column, own_anchor, 0.0)
+        own = tile_of(first_ref[:, :, WIDE:])
+        base = dot(v_ref[...], jnp.concatenate([own, own], axis=0), ((1,), (0,)))
+        made[0] = base + jnp.where(row == column, own_anchor, 0.0)
         store(made.at[0], 0).start()
         store(made.at[0], 0).wait()
 
@@ -281,19 +276,26 @@
             store(zero, k).wait()
 
 
-def band_kernel(place_ref, v_ref, rest_ref, before_ref, out_ref, made, sems):
+def band_kernel(place_ref, v_ref, rest_ref, moved_ref, before_ref, out_ref, made, sems):
     place = place_ref[0]
 
     def store(k):
         return pltpu.make_async_copy(made.at[k - 1], out_ref.at[0, k], sems.at[k - 1])
 
+    def fill(k, block):
+        other = tile_of(block)
+        made[k - 1] = dot(v_ref[...], jnp.concatenate([other, other], axis=0), ((1,), (0,)))
+        store(k).start()
+
+    @pl.when(place == BAND - 1)
+    def _():
+        fill(1, moved_ref[...])
+
     for k in range(1, BAND - 1):
-        @pl.when(k < place)
+        @pl.when((k < place) & (place - k < BAND - 2))
         def _():
             start = pl.multiple_of((place - k - 1) * TILE, TILE)
-            other = tile_of(rest_ref[:, :, pl.ds(start, TILE)])
-            made[k - 1] = dot(v_ref[...], jnp.concatenate([other, other], axis=0), ((1,), (0,)))
-            store(k).start()
+            fill(k, rest_ref[:, :, pl.ds(start, TILE)])
 
     for k in range(1, BAND - 1):
         @pl.when(k < place)
@@ -313,14 +315,9 @@
     prior = prior_precision.reshape(LAYERS, 1)
     send_first = pl.pallas_call(
         first_kernel,
-        out_shape=jax.ShapeDtypeStruct((GROUPS, BAND, 2, WIDE + TILE), BF16),
+        out_shape=pltpu.VMEM((GROUPS, BAND, 2, WIDE + TILE), BF16),
         in_specs=[SMEM, VMEM, VMEM],
-        out_specs=HBM,
-        scratch_shapes=[
-            pltpu.VMEM((GROUPS, 2, WIDE), BF16),
-            pltpu.VMEM((GROUPS, BAND, 2, TILE), BF16),
-            pltpu.SemaphoreType.DMA((BAND + 1,)),
-        ],
+        out_specs=VMEM,
         compiler_params=params(),
         name="first_send",
     )(curvature, jacobian, index)
@@ -340,12 +337,14 @@
     rest = lax.all_to_all(
         send_rest.reshape(DEVICES, 2, REST), AXES, split_axis=0, concat_axis=0, tiled=True
     )
+    pairs = [(h * BAND + BAND - 2, h * BAND + BAND - 1) for h in range(2)]
+    moved = lax.ppermute(first[:, :, WIDE:], "col", pairs)
     parts = TILE // PART
     before, v = pl.pallas_call(
         panel_kernel,
         out_shape=[
             jax.ShapeDtypeStruct((1, BAND, TILE, TILE), F32),
-            jax.ShapeDtypeStruct((TILE, 2 * EXAMPLES), BF16),
+            pltpu.VMEM((TILE, 2 * EXAMPLES), BF16),
         ],
         in_specs=[SMEM, VMEM, VMEM, VMEM],
         out_specs=[HBM, VMEM],
@@ -353,7 +352,7 @@
         + [
             pltpu.VMEM((parts, PART, PART), F32),
             pltpu.VMEM((parts, PART, PART), F32),
-            pltpu.VMEM((parts, PART, PART), F32),
+            pltpu.VMEM((TILE, EXAMPLES), F32),
             pltpu.VMEM((2, TILE, TILE), F32),
             pltpu.VMEM((TILE, TILE), F32),
             pltpu.SemaphoreType.DMA((BAND,)),
@@ -365,16 +364,16 @@
     return pl.pallas_call(
         band_kernel,
         out_shape=jax.ShapeDtypeStruct((1, BAND, TILE, TILE), F32),
-        in_specs=[SMEM, VMEM, VMEM, HBM],
+        in_specs=[SMEM, VMEM, VMEM, VMEM, HBM],
         out_specs=HBM,
         scratch_shapes=[
             pltpu.VMEM((BAND - 2, TILE, TILE), F32),
             pltpu.SemaphoreType.DMA((BAND - 2,)),
         ],
-        input_output_aliases={3: 0},
+        input_output_aliases={4: 0},
         compiler_params=params(),
         name="band",
-    )(place.reshape(1), v, pltpu.with_memory_space_constraint(rest, pltpu.VMEM), before)
+    )(place.reshape(1), pltpu.with_memory_space_constraint(v, pltpu.VMEM), pltpu.with_memory_space_constraint(rest, pltpu.VMEM), pltpu.with_memory_space_constraint(moved, pltpu.VMEM), before)
 
 
 def solution(mesh):

time: 59.4 us -> 56.1 us (0.944)
  Pallas kernels: 24.7 us -> 21.5 us
  waiting for transfers between devices: 16.9 us -> 15.6 us
  starting transfers between devices: 15.4 us -> 16.1 us
    pallas_call x1, Pallas kernels: 16.8 us -> 14.8 us  [body(): pl.pallas_call(panel_kernel, out_shape=[jax.ShapeDtypeStruct((1, BAND, TI...]
    all_to_all x1, waiting for transfers between devices: 7.39 us -> 5.97 us  [body(): lax.all_to_all(send_rest.reshape(DEVICES, 2, REST), AXES, split_axis=0, c...]
    pallas_call x1, Pallas kernels: 3.41 us -> 2.37 us  [body(): pl.pallas_call(band_kernel, out_shape=jax.ShapeDtypeStruct((1, BAND, TILE...]
    ppermute x0 -> x1, starting transfers between devices: none -> 0.68 us  [body(): moved = lax.ppermute(first[:, :, WIDE:], 'col', pairs)]
  transfers between devices with their start and end apart: 2 -> 3, of which waited for: 2 -> 2; matrix products, arithmetic and copies ran while one was open for 3% -> 4% of each run, Pallas kernels for 33% -> 31%
where the time goes in v3:
time: 56.1 us; the launch traced here: 55.4 us
  Pallas kernels  21.5 us (38%)
  starting transfers between devices  16.1 us (29%)
  waiting for transfers between devices  15.6 us (28%)
  local copies, waits for them, and re-layouts  1.52 us (3%)
  other arithmetic  0.65 us (1%)
    pallas_call x1, Pallas kernels, body(): pl.pallas_call(panel_kernel, out_shape=[jax.ShapeDtypeStruct((1, BAND, TI...  14.8 us
    all_to_all x1, starting transfers between devices, body(): lax.all_to_all(send_first.reshape(DEVICES, 2, WIDE + TILE), AXES, split_a...  10.5 us
    all_to_all x1, waiting for transfers between devices, body(): lax.all_to_all(send_first.reshape(DEVICES, 2, WIDE + TILE), AXES, split_a...  9.6 us
    all_to_all x1, waiting for transfers between devices, body(): lax.all_to_all(send_rest.reshape(DEVICES, 2, REST), AXES, split_axis=0, c...  5.97 us
    all_to_all x1, starting transfers between devices, body(): lax.all_to_all(send_rest.reshape(DEVICES, 2, REST), AXES, split_axis=0, c...  4.88 us
    pallas_call x1, Pallas kernels, body(): pl.pallas_call(band_kernel, out_shape=jax.ShapeDtypeStruct((1, BAND, TILE...  2.37 us
    pallas_call x1, Pallas kernels, body(): pl.pallas_call(rest_kernel, out_shape=jax.ShapeDtypeStruct((GROUPS, BAND,...  2.3 us
    pallas_call x1, Pallas kernels, body(): pl.pallas_call(first_kernel, out_shape=pltpu.VMEM((GROUPS, BAND, 2, WIDE...  2.1 us
  transfers between devices with their start and end apart: 3, of which 2 were waited for; matrix products, arithmetic and copies ran while one was open for 4% of the time, Pallas kernels for 31%

profile of v3, /device:TPU:2, one launch (start us, length us, event | category | flops | bytes accessed | tf_op | source)
XLA Modules:
  0.0 55.4 jit_solution(8192943789052282910)
XLA Ops:
  0.0 2.1 %first_send.1 = bf16[16,8,2,1152]{3,2,1,0:T(2,128)(2,1)} custom-call(f32[2]{0:T(128)} %curvature_ref.3, bf16[2,65536]{1,0:T(2,128)(2,1)} %jacobian_ref.3, s32[1,512]{1,0:T(1,128)} %bitcast.7), custom_call_target="tpu_custom_call" | custom-call | tf_op jit(solution)/shard_map/first_send/pallas_call | solution.py:316
  2.1 10.5 %all-to-all-start = ((bf16[128,2,1152]{2,1,0:T(2,128)(2,1)}), bf16[128,2,1152]{2,1,0:T(2,128)(2,1)S(1)}, u32[]{:S(2)}, u32[]{:S(2)}) async-start(bf16[128,2,1152]{2,1,0:T(2,128)(2,1)} %bitcast.3), calls=%async_computation | async-start | bytes 1179648 | tf_op jit(solution)/shard_map/all_to_all | solution.py:324
  12.6 2.3 %rest_send.1 = bf16[16,8,2,2560]{3,2,1,0:T(2,128)(2,1)} custom-call(f32[2]{0:T(128)} %curvature_ref.3, bf16[2,65536]{1,0:T(2,128)(2,1)} %jacobian_ref.3), custom_call_target="tpu_custom_call" | custom-call | tf_op jit(solution)/shard_map/rest_send/pallas_call | solution.py:327
  15.0 1.3 %copy.6.prior_ref = f32[32,1]{1,0:T(8,128)} copy(f32[32,1]{0,1:T(1,128)} %bitcast.9) | data formatting | bytes 256 | tf_op jit(solution)/shard_map/reshape | solution.py:315
  16.3 0.7 %pad_add_fusion.info_ref = s32[2]{0:T(128)} fusion(s32[1]{0:T(128)} %bitcast.place_ref, s32[1]{0:T(128)} %bitcast.1), kind=kLoop, calls=%fused_computation | loop fusion | flops 2 | bytes 16 | tf_op jit(solution)/shard_map/stack | solution.py:363
  16.9 9.6 %all-to-all-done.first_ref = bf16[128,2,1152]{2,1,0:T(2,128)(2,1)S(1)} async-done(((bf16[128,2,1152]{2,1,0:T(2,128)(2,1)}), bf16[128,2,1152]{2,1,0:T(2,128)(2,1)S(1)}, u32[]{:S(2)}, u32[]{:S(2)}) %all-to-all-start) | async-done | bytes 589856 | tf_op jit(solution)/shard_map/all_to_all | solution.py:324
  26.5 4.9 %all-to-all-start.1 = ((bf16[128,2,2560]{2,1,0:T(2,128)(2,1)}), bf16[128,2,2560]{2,1,0:T(2,128)(2,1)S(1)}, u32[]{:S(2)}, u32[]{:S(2)}) async-start(bf16[128,2,2560]{2,1,0:T(2,128)(2,1)} %bitcast.6), calls=%async_computation.1 | async-start | bytes 2621440 | tf_op jit(solution)/shard_map/all_to_all | solution.py:337
  31.4 0.2 slice.3
  31.6 0.7 %collective-permute-start = (bf16[128,2,512]{2,1,0:T(2,128)(2,1)S(1)}, bf16[128,2,512]{2,1,0:T(2,128)(2,1)S(1)}, u32[]{:S(2)}, u32[]{:S(2)}) collective-permute-start(bf16[128,2,512]{2,1,0:T(2,128)(2,1)S(1)} %slice.3), channel_id=1, source_target_pairs={{6,7},{14,15},{22,23},{30,31},{38,39},{46,47},{54,55},{62,63},{70,... | collective-permute-start | bytes 786440 | tf_op jit(solution)/shard_map/ppermute | solution.py:341
  32.3 14.8 %panel.1 = (f32[1,8,512,512]{3,2,1,0:T(8,128)}, bf16[512,512]{1,0:T(8,128)(2,1)S(1)}) custom-call(s32[2]{0:T(128)} %pad_add_fusion.info_ref, bf16[128,2,1152]{2,1,0:T(2,128)(2,1)S(1)} %all-to-all-done.first_ref, s32[1,512]{1,0:T(1,128)} %bitcast.8, f32[32,1]{1,0:T(8,128)} %copy.6.prior_ref), custom_call_target="tpu_custom_call" | custom-call | flops 20000000000 | bytes 2000000 | tf_op jit(solution)/shard_map/panel/pallas_call | solution.py:343
  47.1 0.0 collective-permute-done.moved_ref
  47.1 6.0 %all-to-all-done.1.rest_ref = bf16[128,2,2560]{2,1,0:T(2,128)(2,1)S(1)} async-done(((bf16[128,2,2560]{2,1,0:T(2,128)(2,1)}), bf16[128,2,2560]{2,1,0:T(2,128)(2,1)S(1)}, u32[]{:S(2)}, u32[]{:S(2)}) %all-to-all-start.1) | async-done | bytes 1310752 | tf_op jit(solution)/shard_map/all_to_all | solution.py:337
  53.1 2.4 %band.1 = f32[1,8,512,512]{3,2,1,0:T(8,128)} custom-call(s32[1]{0:T(128)} %bitcast.place_ref, bf16[512,512]{1,0:T(8,128)(2,1)S(1)} %get-tuple-element.10.v_ref, bf16[128,2,2560]{2,1,0:T(2,128)(2,1)S(1)} %all-to-all-done.1.rest_ref, bf16[128,2,512]{2,1,0:T(2,128)(2,1)S(1)} %collective-permute-done.moved_ref, ...), custom_call_target="tpu_custom_call", output_to_operand_aliasing={{}: (4, {})} | custom-call | tf_op jit(solution)/shard_map/band/pallas_call | solution.py:364
Async XLA Ops:
  2.1 24.4 %all-to-all-start = ((bf16[128,2,1152]{2,1,0:T(2,128)(2,1)}), bf16[128,2,1152]{2,1,0:T(2,128)(2,1)S(1)}, u32[]{:S(2)}, u32[]{:S(2)}) async-start(bf16[128,2,1152]{2,1,0:T(2,128)(2,1)} %bitcast.3), calls=%async_computation | async-start | bytes 1179648 | tf_op jit(solution)/shard_map/all_to_all | solution.py:324
  26.5 26.5 %all-to-all-start.1 = ((bf16[128,2,2560]{2,1,0:T(2,128)(2,1)}), bf16[128,2,2560]{2,1,0:T(2,128)(2,1)S(1)}, u32[]{:S(2)}, u32[]{:S(2)}) async-start(bf16[128,2,2560]{2,1,0:T(2,128)(2,1)} %bitcast.6), calls=%async_computation.1 | async-start | bytes 2621440 | tf_op jit(solution)/shard_map/all_to_all | solution.py:337
  31.6 15.5 %collective-permute-start = (bf16[128,2,512]{2,1,0:T(2,128)(2,1)S(1)}, bf16[128,2,512]{2,1,0:T(2,128)(2,1)S(1)}, u32[]{:S(2)}, u32[]{:S(2)}) collective-permute-start(bf16[128,2,512]{2,1,0:T(2,128)(2,1)S(1)} %slice.3), channel_id=1, source_target_pairs={{6,7},{14,15},{22,23},{30,31},{38,39},{46,47},{54,55},{62,63},{70,... | collective-permute-start | bytes 786440 | tf_op jit(solution)/shard_map/ppermute | solution.py:341

commit v4 on v3

--- a/solution.py
+++ b/solution.py
@@ -13,7 +13,9 @@
 DEVICES = 128
 EXAMPLES = 256
 WIDE = TILE + 128
-REST = (BAND - 3) * TILE
+SENT = 5
+REST = SENT * TILE
+STEPS = BAND - 2 - SENT
 PART = 128
 F32 = jnp.float32
 BF16 = jnp.bfloat16
@@ -169,14 +171,18 @@
 
 
 def layer_anchor(low, high, at, prior_ref):
+    row = lax.broadcasted_iota(jnp.int32, (LAYERS, LAYERS), 0)
+    column = lax.broadcasted_iota(jnp.int32, (LAYERS, LAYERS), 1)
+    prior = jnp.sum(jnp.where(row == column, prior_ref[...], 0.0), axis=1, keepdims=True)
     inside = (at >= low) & (at < high)
-    return jnp.sum(jnp.where(inside, prior_ref[...], 0.0), axis=0, keepdims=True)
-
-
-def panel_kernel(info_ref, first_ref, index_ref, prior_ref, out_ref, v_ref, *scratch):
+    return jnp.sum(jnp.where(inside, prior, 0.0), axis=0, keepdims=True)
+
+
+def panel_kernel(position_ref, first_ref, index_ref, prior_ref, out_ref, v_ref, *scratch):
     parts = TILE // PART
     r_refs, (t_ref, f_ref, z_ref, made, zero, sems) = scratch[:parts], scratch[parts:]
-    lead, place = info_ref[0], info_ref[1]
+    place = lax.rem(position_ref[0], BAND)
+    lead = position_ref[0] - place
 
     def store(source, k):
         return pltpu.make_async_copy(source, out_ref.at[0, k], sems.at[k])
@@ -276,31 +282,43 @@
             store(zero, k).wait()
 
 
-def band_kernel(place_ref, v_ref, rest_ref, moved_ref, before_ref, out_ref, made, sems):
-    place = place_ref[0]
-
-    def store(k):
-        return pltpu.make_async_copy(made.at[k - 1], out_ref.at[0, k], sems.at[k - 1])
-
-    def fill(k, block):
-        other = tile_of(block)
-        made[k - 1] = dot(v_ref[...], jnp.concatenate([other, other], axis=0), ((1,), (0,)))
-        store(k).start()
-
-    @pl.when(place == BAND - 1)
-    def _():
-        fill(1, moved_ref[...])
-
-    for k in range(1, BAND - 1):
-        @pl.when((k < place) & (place - k < BAND - 2))
+def write_slots(v_ref, out_ref, made, sems, cases):
+    def store(n, k):
+        return pltpu.make_async_copy(made.at[n], out_ref.at[0, k], sems.at[n])
+
+    for n, (k, wanted, block) in enumerate(cases):
+        @pl.when(wanted)
         def _():
-            start = pl.multiple_of((place - k - 1) * TILE, TILE)
-            fill(k, rest_ref[:, :, pl.ds(start, TILE)])
-
-    for k in range(1, BAND - 1):
-        @pl.when(k < place)
+            other = tile_of(block())
+            made[n] = dot(v_ref[...], jnp.concatenate([other, other], axis=0), ((1,), (0,)))
+            store(n, k).start()
+
+    for n, (k, wanted, block) in enumerate(cases):
+        @pl.when(wanted)
         def _():
-            store(k).wait()
+            store(n, k).wait()
+
+
+def band_kernel(position_ref, v_ref, rest_ref, before_ref, out_ref, made, sems):
+    place = lax.rem(position_ref[0], BAND)
+
+    def block(k):
+        start = pl.multiple_of((place - k - 1) * TILE, TILE)
+        return lambda: rest_ref[:, :, pl.ds(start, TILE)]
+
+    cases = [(k, (k < place) & (place - k <= SENT), block(k)) for k in range(1, BAND - 1)]
+    write_slots(v_ref, out_ref, made, sems, cases)
+
+
+def moved_kernel(position_ref, v_ref, before_ref, *rest):
+    moved, (out_ref, made, sems) = rest[:STEPS], rest[STEPS:]
+    place = lax.rem(position_ref[0], BAND)
+    cases = [(k, place - k > SENT, lambda k=k: moved[k - 1][...]) for k in range(1, STEPS + 1)]
+    write_slots(v_ref, out_ref, made, sems, cases)
+
+
+def close(x):
+    return pltpu.with_memory_space_constraint(x, pltpu.VMEM)
 
 
 SMEM = pl.BlockSpec(memory_space=pltpu.SMEM)
@@ -310,9 +328,8 @@
 
 def body(jacobian, curvature, sub_index, prior_precision):
     position = lax.axis_index(AXES).astype(jnp.int32)
-    place = lax.rem(position, BAND)
     index = sub_index.reshape(1, TILE)
-    prior = prior_precision.reshape(LAYERS, 1)
+    prior = prior_precision.reshape(1, LAYERS)
     send_first = pl.pallas_call(
         first_kernel,
         out_shape=pltpu.VMEM((GROUPS, BAND, 2, WIDE + TILE), BF16),
@@ -337,8 +354,12 @@
     rest = lax.all_to_all(
         send_rest.reshape(DEVICES, 2, REST), AXES, split_axis=0, concat_axis=0, tiled=True
     )
-    pairs = [(h * BAND + BAND - 2, h * BAND + BAND - 1) for h in range(2)]
-    moved = lax.ppermute(first[:, :, WIDE:], "col", pairs)
+    moved = []
+    for step in range(STEPS, 0, -1):
+        pairs = [
+            (h * BAND + i, h * BAND + i + step) for h in range(2) for i in range(SENT + 1, BAND - step)
+        ]
+        moved.insert(0, lax.ppermute(first[:, :, WIDE:], "col", pairs))
     parts = TILE // PART
     before, v = pl.pallas_call(
         panel_kernel,
@@ -358,22 +379,30 @@
             pltpu.SemaphoreType.DMA((BAND,)),
         ],
         compiler_params=params(),
-        cost_estimate=pl.CostEstimate(flops=2 * 10**10, bytes_accessed=2 * 10**6, transcendentals=10**6),
+        cost_estimate=pl.CostEstimate(flops=2 * 10**9, bytes_accessed=2 * 10**6, transcendentals=10**6),
         name="panel",
-    )(jnp.stack([position - place, place]), pltpu.with_memory_space_constraint(first, pltpu.VMEM), index, prior)
-    return pl.pallas_call(
+    )(position.reshape(1), pltpu.with_memory_space_constraint(first, pltpu.VMEM), index, prior)
+    slots = jax.ShapeDtypeStruct((1, BAND, TILE, TILE), F32)
+    before = pl.pallas_call(
         band_kernel,
-        out_shape=jax.ShapeDtypeStruct((1, BAND, TILE, TILE), F32),
-        in_specs=[SMEM, VMEM, VMEM, VMEM, HBM],
+        out_shape=slots,
+        in_specs=[SMEM, VMEM, VMEM, HBM],
         out_specs=HBM,
-        scratch_shapes=[
-            pltpu.VMEM((BAND - 2, TILE, TILE), F32),
-            pltpu.SemaphoreType.DMA((BAND - 2,)),
-        ],
-        input_output_aliases={4: 0},
+        scratch_shapes=[pltpu.VMEM((BAND - 2, TILE, TILE), F32), pltpu.SemaphoreType.DMA((BAND - 2,))],
+        input_output_aliases={3: 0},
         compiler_params=params(),
         name="band",
-    )(place.reshape(1), pltpu.with_memory_space_constraint(v, pltpu.VMEM), pltpu.with_memory_space_constraint(rest, pltpu.VMEM), pltpu.with_memory_space_constraint(moved, pltpu.VMEM), before)
+    )(position.reshape(1), close(v), close(rest), before)
+    return pl.pallas_call(
+        moved_kernel,
+        out_shape=slots,
+        in_specs=[SMEM, VMEM, HBM] + [VMEM] * STEPS,
+        out_specs=HBM,
+        scratch_shapes=[pltpu.VMEM((STEPS, TILE, TILE), F32), pltpu.SemaphoreType.DMA((STEPS,))],
+        input_output_aliases={2: 0},
+        compiler_params=params(),
+        name="moved",
+    )(position.reshape(1), close(v), before, *[close(x) for x in moved])
 
 
 def solution(mesh):

time: 56.1 us -> 55.8 us (level)
  waiting for transfers between devices: 15.6 us -> 17.7 us
  local copies, waits for them, and re-layouts: 1.52 us -> 0.18 us
  other arithmetic: 0.65 us -> 0 us
    all_to_all x1, waiting for transfers between devices: 9.6 us -> 11.6 us  [body(): lax.all_to_all(send_first.reshape(DEVICES, 2, WIDE + TILE), AXES, split_a...]
    reshape x1 -> x0, local copies, waits for them, and re-layouts: 1.34 us -> none  [body(): prior = prior_precision.reshape(LAYERS, 1)]
    another operation x1 -> x0, other arithmetic: 0.65 us -> none  [body(): jnp.stack([position - place, place])]
    pallas_call x1 -> x2, Pallas kernels: 2.37 us -> 2.39 us  [the longest x1 2.37 us: body(): pl.pallas_call(band_kernel, out_shape=slots, in_specs=[SMEM, VMEM, VMEM,...]
  transfers between devices with their start and end apart: 3 -> 3, of which waited for: 2 -> 2; matrix products, arithmetic and copies ran while one was open for 4% -> 0% of each run, Pallas kernels for 31% -> 35%
where the time goes in v4:
time: 55.8 us; the launch traced here: 55.5 us
  Pallas kernels  21.4 us (38%)
  waiting for transfers between devices  17.7 us (32%)
  starting transfers between devices  16.1 us (29%)
    pallas_call x1, Pallas kernels, body(): pl.pallas_call(panel_kernel, out_shape=[jax.ShapeDtypeStruct((1, BAND, TI...  14.6 us
    all_to_all x1, waiting for transfers between devices, body(): lax.all_to_all(send_first.reshape(DEVICES, 2, WIDE + TILE), AXES, split_a...  11.6 us
    all_to_all x1, starting transfers between devices, body(): lax.all_to_all(send_first.reshape(DEVICES, 2, WIDE + TILE), AXES, split_a...  10.5 us
    all_to_all x1, waiting for transfers between devices, body(): lax.all_to_all(send_rest.reshape(DEVICES, 2, REST), AXES, split_axis=0, c...  6.11 us
    all_to_all x1, starting transfers between devices, body(): lax.all_to_all(send_rest.reshape(DEVICES, 2, REST), AXES, split_axis=0, c...  4.88 us
    pallas_call x1, Pallas kernels, body(): pl.pallas_call(band_kernel, out_shape=slots, in_specs=[SMEM, VMEM, VMEM,...  2.37 us
    pallas_call x1, Pallas kernels, body(): pl.pallas_call(rest_kernel, out_shape=jax.ShapeDtypeStruct((GROUPS, BAND,...  2.3 us
    pallas_call x1, Pallas kernels, body(): pl.pallas_call(first_kernel, out_shape=pltpu.VMEM((GROUPS, BAND, 2, WIDE...  2.1 us
  transfers between devices with their start and end apart: 3, of which 2 were waited for; matrix products, arithmetic and copies ran while one was open for 0% of the time, Pallas kernels for 35%

profile of v4, /device:TPU:2, one launch (start us, length us, event | category | flops | bytes accessed | tf_op | source)
XLA Modules:
  0.0 55.5 jit_solution(5948662291841320396)
XLA Ops:
  0.0 2.1 %first_send.1 = bf16[16,8,2,1152]{3,2,1,0:T(2,128)(2,1)} custom-call(f32[2]{0:T(128)} %curvature_ref.3, bf16[2,65536]{1,0:T(2,128)(2,1)} %jacobian_ref.3, s32[1,512]{1,0:T(1,128)} %bitcast.6), custom_call_target="tpu_custom_call" | custom-call | tf_op jit(solution)/shard_map/first_send/pallas_call | solution.py:333
  2.1 10.5 %all-to-all-start = ((bf16[128,2,1152]{2,1,0:T(2,128)(2,1)}), bf16[128,2,1152]{2,1,0:T(2,128)(2,1)S(1)}, u32[]{:S(2)}, u32[]{:S(2)}) async-start(bf16[128,2,1152]{2,1,0:T(2,128)(2,1)} %bitcast.2), calls=%async_computation | async-start | bytes 1179648 | tf_op jit(solution)/shard_map/all_to_all | solution.py:341
  12.6 2.3 %rest_send.1 = bf16[16,8,2,2560]{3,2,1,0:T(2,128)(2,1)} custom-call(f32[2]{0:T(128)} %curvature_ref.3, bf16[2,65536]{1,0:T(2,128)(2,1)} %jacobian_ref.3), custom_call_target="tpu_custom_call" | custom-call | tf_op jit(solution)/shard_map/rest_send/pallas_call | solution.py:344
  14.9 11.6 %all-to-all-done.first_ref = bf16[128,2,1152]{2,1,0:T(2,128)(2,1)S(1)} async-done(((bf16[128,2,1152]{2,1,0:T(2,128)(2,1)}), bf16[128,2,1152]{2,1,0:T(2,128)(2,1)S(1)}, u32[]{:S(2)}, u32[]{:S(2)}) %all-to-all-start) | async-done | bytes 589856 | tf_op jit(solution)/shard_map/all_to_all | solution.py:341
  26.5 4.9 %all-to-all-start.1 = ((bf16[128,2,2560]{2,1,0:T(2,128)(2,1)}), bf16[128,2,2560]{2,1,0:T(2,128)(2,1)S(1)}, u32[]{:S(2)}, u32[]{:S(2)}) async-start(bf16[128,2,2560]{2,1,0:T(2,128)(2,1)} %bitcast.5), calls=%async_computation.1 | async-start | bytes 2621440 | tf_op jit(solution)/shard_map/all_to_all | solution.py:354
  31.4 0.2 slice.3
  31.6 0.7 %collective-permute-start = (bf16[128,2,512]{2,1,0:T(2,128)(2,1)S(1)}, bf16[128,2,512]{2,1,0:T(2,128)(2,1)S(1)}, u32[]{:S(2)}, u32[]{:S(2)}) collective-permute-start(bf16[128,2,512]{2,1,0:T(2,128)(2,1)S(1)} %slice.3), channel_id=1, source_target_pairs={{6,7},{14,15},{22,23},{30,31},{38,39},{46,47},{54,55},{62,63},{70,... | collective-permute-start | bytes 786440 | tf_op jit(solution)/shard_map/ppermute | solution.py:362
  32.3 14.6 %panel.1 = (f32[1,8,512,512]{3,2,1,0:T(8,128)}, bf16[512,512]{1,0:T(8,128)(2,1)S(1)}) custom-call(s32[1]{0:T(128)} %bitcast.position_ref, bf16[128,2,1152]{2,1,0:T(2,128)(2,1)S(1)} %all-to-all-done.first_ref, s32[1,512]{1,0:T(1,128)} %bitcast.7, f32[1,32]{1,0:T(1,128)} %bitcast.8), custom_call_target="tpu_custom_call" | custom-call | flops 2000000000 | bytes 2000000 | tf_op jit(solution)/shard_map/panel/pallas_call | solution.py:364
  47.0 6.1 %all-to-all-done.1.rest_ref = bf16[128,2,2560]{2,1,0:T(2,128)(2,1)S(1)} async-done(((bf16[128,2,2560]{2,1,0:T(2,128)(2,1)}), bf16[128,2,2560]{2,1,0:T(2,128)(2,1)S(1)}, u32[]{:S(2)}, u32[]{:S(2)}) %all-to-all-start.1) | async-done | bytes 1310752 | tf_op jit(solution)/shard_map/all_to_all | solution.py:354
  53.1 2.4 %band.1.before_ref = f32[1,8,512,512]{3,2,1,0:T(8,128)} custom-call(s32[1]{0:T(128)} %bitcast.position_ref, bf16[512,512]{1,0:T(8,128)(2,1)S(1)} %get-tuple-element.10.v_ref, bf16[128,2,2560]{2,1,0:T(2,128)(2,1)S(1)} %all-to-all-done.1.rest_ref, f32[1,8,512,512]{3,2,1,0:T(8,128)} %get-tuple-element.12.before_ref), custom_call_target="tpu_custom_call", output_to_operand_aliasing={{}: (3, {})} | custom-call | tf_op jit(solution)/shard_map/band/pallas_call | solution.py:386
  55.4 0.0 collective-permute-done.rest_0_
  (1 shorter events, 0.0 us)
Async XLA Ops:
  2.1 24.4 %all-to-all-start = ((bf16[128,2,1152]{2,1,0:T(2,128)(2,1)}), bf16[128,2,1152]{2,1,0:T(2,128)(2,1)S(1)}, u32[]{:S(2)}, u32[]{:S(2)}) async-start(bf16[128,2,1152]{2,1,0:T(2,128)(2,1)} %bitcast.2), calls=%async_computation | async-start | bytes 1179648 | tf_op jit(solution)/shard_map/all_to_all | solution.py:341
  26.5 26.5 %all-to-all-start.1 = ((bf16[128,2,2560]{2,1,0:T(2,128)(2,1)}), bf16[128,2,2560]{2,1,0:T(2,128)(2,1)S(1)}, u32[]{:S(2)}, u32[]{:S(2)}) async-start(bf16[128,2,2560]{2,1,0:T(2,128)(2,1)} %bitcast.5), calls=%async_computation.1 | async-start | bytes 2621440 | tf_op jit(solution)/shard_map/all_to_all | solution.py:354
  31.6 23.8 %collective-permute-start = (bf16[128,2,512]{2,1,0:T(2,128)(2,1)S(1)}, bf16[128,2,512]{2,1,0:T(2,128)(2,1)S(1)}, u32[]{:S(2)}, u32[]{:S(2)}) collective-permute-start(bf16[128,2,512]{2,1,0:T(2,128)(2,1)S(1)} %slice.3), channel_id=1, source_target_pairs={{6,7},{14,15},{22,23},{30,31},{38,39},{46,47},{54,55},{62,63},{70,... | collective-permute-start | bytes 786440 | tf_op jit(solution)/shard_map/ppermute | solution.py:362

commit v5 on v4

--- a/solution.py
+++ b/solution.py
@@ -13,7 +13,7 @@
 DEVICES = 128
 EXAMPLES = 256
 WIDE = TILE + 128
-SENT = 5
+SENT = 4
 REST = SENT * TILE
 STEPS = BAND - 2 - SENT
 PART = 128
@@ -283,20 +283,27 @@
 
 
 def write_slots(v_ref, out_ref, made, sems, cases):
-    def store(n, k):
-        return pltpu.make_async_copy(made.at[n], out_ref.at[0, k], sems.at[n])
+    half = TILE // 2
+
+    def store(n, k, part):
+        rows = pl.ds(part * half, half)
+        return pltpu.make_async_copy(made.at[n, rows], out_ref.at[0, k, rows], sems.at[n, part])
 
     for n, (k, wanted, block) in enumerate(cases):
         @pl.when(wanted)
         def _():
             other = tile_of(block())
-            made[n] = dot(v_ref[...], jnp.concatenate([other, other], axis=0), ((1,), (0,)))
-            store(n, k).start()
+            pair = jnp.concatenate([other, other], axis=0)
+            for part in range(2):
+                rows = slice(part * half, (part + 1) * half)
+                made[n, rows] = dot(v_ref[rows, :], pair, ((1,), (0,)))
+                store(n, k, part).start()
 
     for n, (k, wanted, block) in enumerate(cases):
         @pl.when(wanted)
         def _():
-            store(n, k).wait()
+            for part in range(2):
+                store(n, k, part).wait()
 
 
 def band_kernel(position_ref, v_ref, rest_ref, before_ref, out_ref, made, sems):
@@ -388,7 +395,7 @@
         out_shape=slots,
         in_specs=[SMEM, VMEM, VMEM, HBM],
         out_specs=HBM,
-        scratch_shapes=[pltpu.VMEM((BAND - 2, TILE, TILE), F32), pltpu.SemaphoreType.DMA((BAND - 2,))],
+        scratch_shapes=[pltpu.VMEM((BAND - 2, TILE, TILE), F32), pltpu.SemaphoreType.DMA((BAND - 2, 2))],
         input_output_aliases={3: 0},
         compiler_params=params(),
         name="band",
@@ -398,7 +405,7 @@
         out_shape=slots,
         in_specs=[SMEM, VMEM, HBM] + [VMEM] * STEPS,
         out_specs=HBM,
-        scratch_shapes=[pltpu.VMEM((STEPS, TILE, TILE), F32), pltpu.SemaphoreType.DMA((STEPS,))],
+        scratch_shapes=[pltpu.VMEM((STEPS, TILE, TILE), F32), pltpu.SemaphoreType.DMA((STEPS, 2))],
         input_output_aliases={2: 0},
         compiler_params=params(),
         name="moved",

time: 55.8 us -> 55.4 us (level)
  the two profiles are of different devices: /device:TPU:2 before, /device:TPU:35 now
where the time goes in v5:
time: 55.4 us; the launch traced here: 55.1 us
  starting transfers between devices  22.9 us (41%)
  Pallas kernels  21.7 us (39%)
  waiting for transfers between devices  10.1 us (18%)
    pallas_call x1, Pallas kernels, body(): pl.pallas_call(panel_kernel, out_shape=[jax.ShapeDtypeStruct((1, BAND, TI...  14.6 us
    all_to_all x1, starting transfers between devices, body(): lax.all_to_all(send_first.reshape(DEVICES, 2, WIDE + TILE), AXES, split_a...  10.5 us
    all_to_all x1, waiting for transfers between devices, body(): lax.all_to_all(send_first.reshape(DEVICES, 2, WIDE + TILE), AXES, split_a...  10.1 us
    all_to_all x1, starting transfers between devices, body(): lax.all_to_all(send_rest.reshape(DEVICES, 2, REST), AXES, split_axis=0, c...  6.68 us
    ppermute x2, starting transfers between devices, body(): moved.insert(0, lax.ppermute(first[:, :, WIDE:], 'col', pairs))  5.73 us
    pallas_call x1, Pallas kernels, body(): pl.pallas_call(band_kernel, out_shape=slots, in_specs=[SMEM, VMEM, VMEM,...  2.75 us
    pallas_call x1, Pallas kernels, body(): pl.pallas_call(rest_kernel, out_shape=jax.ShapeDtypeStruct((GROUPS, BAND,...  2.17 us
    pallas_call x1, Pallas kernels, body(): pl.pallas_call(first_kernel, out_shape=pltpu.VMEM((GROUPS, BAND, 2, WIDE...  2.1 us
  transfers between devices with their start and end apart: 4, of which 1 were waited for; matrix products, arithmetic and copies ran while one was open for 0% of the time, Pallas kernels for 35%

profile of v5, /device:TPU:35, one launch (start us, length us, event | category | flops | bytes accessed | tf_op | source)
XLA Modules:
  0.0 55.1 jit_solution(10520073618945588425)
XLA Ops:
  0.0 2.1 %first_send.1 = bf16[16,8,2,1152]{3,2,1,0:T(2,128)(2,1)} custom-call(f32[2]{0:T(128)} %curvature_ref.3, bf16[2,65536]{1,0:T(2,128)(2,1)} %jacobian_ref.3, s32[1,512]{1,0:T(1,128)} %bitcast.6), custom_call_target="tpu_custom_call" | custom-call | tf_op jit(solution)/shard_map/first_send/pallas_call | solution.py:340
  2.1 10.5 %all-to-all-start = ((bf16[128,2,1152]{2,1,0:T(2,128)(2,1)}), bf16[128,2,1152]{2,1,0:T(2,128)(2,1)S(1)}, u32[]{:S(2)}, u32[]{:S(2)}) async-start(bf16[128,2,1152]{2,1,0:T(2,128)(2,1)} %bitcast.2), calls=%async_computation | async-start | bytes 1179648 | tf_op jit(solution)/shard_map/all_to_all | solution.py:348
  12.6 2.2 %rest_send.1 = bf16[16,8,2,2048]{3,2,1,0:T(2,128)(2,1)} custom-call(f32[2]{0:T(128)} %curvature_ref.3, bf16[2,65536]{1,0:T(2,128)(2,1)} %jacobian_ref.3), custom_call_target="tpu_custom_call" | custom-call | tf_op jit(solution)/shard_map/rest_send/pallas_call | solution.py:351
  14.8 10.1 %all-to-all-done.first_ref = bf16[128,2,1152]{2,1,0:T(2,128)(2,1)S(1)} async-done(((bf16[128,2,1152]{2,1,0:T(2,128)(2,1)}), bf16[128,2,1152]{2,1,0:T(2,128)(2,1)S(1)}, u32[]{:S(2)}, u32[]{:S(2)}) %all-to-all-start) | async-done | bytes 589856 | tf_op jit(solution)/shard_map/all_to_all | solution.py:348
  24.9 6.7 %all-to-all-start.1 = ((bf16[128,2,2048]{2,1,0:T(2,128)(2,1)}), bf16[128,2,2048]{2,1,0:T(2,128)(2,1)S(1)}, u32[]{:S(2)}, u32[]{:S(2)}) async-start(bf16[128,2,2048]{2,1,0:T(2,128)(2,1)} %bitcast.5), calls=%async_computation.1 | async-start | bytes 2097152 | tf_op jit(solution)/shard_map/all_to_all | solution.py:361
  31.6 0.2 slice.4
  31.8 4.2 %collective-permute-start.1 = (bf16[128,2,512]{2,1,0:T(2,128)(2,1)S(1)}, bf16[128,2,512]{2,1,0:T(2,128)(2,1)S(1)}, u32[]{:S(2)}, u32[]{:S(2)}) collective-permute-start(bf16[128,2,512]{2,1,0:T(2,128)(2,1)S(1)} %slice.4), channel_id=1, source_target_pairs={{5,7},{13,15},{21,23},{29,31},{37,39},{45,47},{53,55},{61,63},{69,... | collective-permute-start | bytes 786440 | tf_op jit(solution)/shard_map/ppermute | solution.py:369
  36.0 1.5 %collective-permute-start = (bf16[128,2,512]{2,1,0:T(2,128)(2,1)S(1)}, bf16[128,2,512]{2,1,0:T(2,128)(2,1)S(1)}, u32[]{:S(2)}, u32[]{:S(2)}) collective-permute-start(bf16[128,2,512]{2,1,0:T(2,128)(2,1)S(1)} %slice.4), channel_id=1, source_target_pairs={{5,6},{6,7},{13,14},{14,15},{21,22},{22,23},{29,30},{30,31},{37,38... | collective-permute-start | bytes 786440 | tf_op jit(solution)/shard_map/ppermute | solution.py:369
  37.5 14.6 %panel.1 = (f32[1,8,512,512]{3,2,1,0:T(8,128)}, bf16[512,512]{1,0:T(8,128)(2,1)S(1)}) custom-call(s32[1]{0:T(128)} %bitcast.position_ref, bf16[128,2,1152]{2,1,0:T(2,128)(2,1)S(1)} %all-to-all-done.first_ref, s32[1,512]{1,0:T(1,128)} %bitcast.7, f32[1,32]{1,0:T(1,128)} %bitcast.8), custom_call_target="tpu_custom_call" | custom-call | flops 2000000000 | bytes 2000000 | tf_op jit(solution)/shard_map/panel/pallas_call | solution.py:371
  52.1 0.0 all-to-all-done.1.rest_ref
  52.1 2.7 %band.1.before_ref = f32[1,8,512,512]{3,2,1,0:T(8,128)} custom-call(s32[1]{0:T(128)} %bitcast.position_ref, bf16[512,512]{1,0:T(8,128)(2,1)S(1)} %get-tuple-element.10.v_ref, bf16[128,2,2048]{2,1,0:T(2,128)(2,1)S(1)} %all-to-all-done.1.rest_ref, f32[1,8,512,512]{3,2,1,0:T(8,128)} %get-tuple-element.12.before_ref), custom_call_target="tpu_custom_call", output_to_operand_aliasing={{}: (3, {})} | custom-call | tf_op jit(solution)/shard_map/band/pallas_call | solution.py:393
  54.9 0.0 collective-permute-done.1.rest_1_
  54.9 0.0 collective-permute-done.rest_0_
  54.9 0.1 moved.1
Async XLA Ops:
  2.1 22.8 %all-to-all-start = ((bf16[128,2,1152]{2,1,0:T(2,128)(2,1)}), bf16[128,2,1152]{2,1,0:T(2,128)(2,1)S(1)}, u32[]{:S(2)}, u32[]{:S(2)}) async-start(bf16[128,2,1152]{2,1,0:T(2,128)(2,1)} %bitcast.2), calls=%async_computation | async-start | bytes 1179648 | tf_op jit(solution)/shard_map/all_to_all | solution.py:348
  24.9 27.3 %all-to-all-start.1 = ((bf16[128,2,2048]{2,1,0:T(2,128)(2,1)}), bf16[128,2,2048]{2,1,0:T(2,128)(2,1)S(1)}, u32[]{:S(2)}, u32[]{:S(2)}) async-start(bf16[128,2,2048]{2,1,0:T(2,128)(2,1)} %bitcast.5), calls=%async_computation.1 | async-start | bytes 2097152 | tf_op jit(solution)/shard_map/all_to_all | solution.py:361
  31.8 23.2 %collective-permute-start.1 = (bf16[128,2,512]{2,1,0:T(2,128)(2,1)S(1)}, bf16[128,2,512]{2,1,0:T(2,128)(2,1)S(1)}, u32[]{:S(2)}, u32[]{:S(2)}) collective-permute-start(bf16[128,2,512]{2,1,0:T(2,128)(2,1)S(1)} %slice.4), channel_id=1, source_target_pairs={{5,7},{13,15},{21,23},{29,31},{37,39},{45,47},{53,55},{61,63},{69,... | collective-permute-start | bytes 786440 | tf_op jit(solution)/shard_map/ppermute | solution.py:369
  36.0 18.9 %collective-permute-start = (bf16[128,2,512]{2,1,0:T(2,128)(2,1)S(1)}, bf16[128,2,512]{2,1,0:T(2,128)(2,1)S(1)}, u32[]{:S(2)}, u32[]{:S(2)}) collective-permute-start(bf16[128,2,512]{2,1,0:T(2,128)(2,1)S(1)} %slice.4), channel_id=1, source_target_pairs={{5,6},{6,7},{13,14},{14,15},{21,22},{22,23},{29,30},{30,31},{37,38... | collective-permute-start | bytes 786440 | tf_op jit(solution)/shard_map/ppermute | solution.py:369
